TPU v7x, 512 devices: a whole 4x4x16 slice. The times are simulated.
512 devices in a mesh: role: 4 (over y), pairs: 128 (over x, z, core).
Axes of the slice: x: 4, y: 4, z: 16, core: 2. Of those that a mesh axis runs over, the one named last changes fastest.
Arguments:
- three_index: bfloat16 [256, 1024, 512], P('pairs'), may hold values from -6 to 6
- coeff: bfloat16 [512, 512, 256], P('pairs'), may hold values from -6 to 6
- amps: bfloat16 [512, 256, 256], P('pairs'), may hold values from -4 to 4
- eps_virt: float32 [512, 256], P('pairs'), may hold values from 0.3 to 3
- eps_occ: float32 [256], replicated, may hold values from -1.5 to -0.3
- nvirt: int32 [512], P('pairs'), may hold values from 64 to 256, as said below
- pair_occ: int32 [512, 2], P('pairs'), may hold values from 0 to 255, as said below
- partners: int32 [512, 8], P('pairs'), may hold values from 0 to 511, as said below
- coupling: float32 [512, 8], P('pairs'), may hold values from -1 to 1
- pair_owner: int32 [512], P('pairs'), may hold values from 1 to 3, as said below
Outputs:
- amps_out: bfloat16 [1024, 256, 256], P(('role', 'pairs'))
- dressed_out: bfloat16 [1024, 512, 256], P(('role', 'pairs'))
Inputs may be any that keep to these rules, and one draw needn't show every extreme that they name: `nvirt`: each block of 4 consecutive pairs has one pair with all 256 virtuals. `pair_occ`: for pair k in block c = k // 4, the first orbital is one of the 2 orbitals numbered from 2 * c, and the second is one of the 6 orbitals numbered cyclically from 2 * (c - 1) modulo 256. Pair k's partners are distinct pairs of its own block of 4 pairs and the blocks just before and after it, cyclically modulo 512. `pair_owner`: in each block of 4 consecutive pairs, each of the roles 1 to 3 holds one or two pairs and exactly one role holds two.
All inputs are finite; a program needn't handle non-finite values.
Results may differ from a plain program's by a relative error of at most 0.012.
Values may be sent and summed in bfloat16 or wider, within the bound.
A program may use at most 64 MiB of HBM per device.

v0:
```python
import math

import jax
import jax.numpy as jnp
from jax import lax
from jax.sharding import PartitionSpec as P

PARTNERS = 8
ITERS = 2
SLOTS = 2


def extended(cells, sides, width):
    for axis, dim in sides:
        count = lax.axis_size(axis)
        head = lax.slice_in_dim(cells, 0, width, axis=dim)
        tail = lax.slice_in_dim(cells, cells.shape[dim] - width, cells.shape[dim], axis=dim)
        cells = jnp.concatenate(
            [
                lax.ppermute(tail, axis, [(i, (i + 1) % count) for i in range(count)]),
                cells,
                lax.ppermute(head, axis, [((i + 1) % count, i) for i in range(count)]),
            ],
            axis=dim,
        )
    return cells


def from_root(value, axis, source):
    kept = jnp.where(lax.axis_index(axis) == source, value, 0).astype(value.dtype)
    return lax.psum(kept, axis)


def local(
    three_index, coeff, amps, eps_virt, eps_occ, nvirt, pair_occ, partners, coupling, pair_owner
):
    column_count = lax.axis_size("pairs")
    role_index = lax.axis_index("role")
    column = lax.axis_index("pairs")
    occ_block = three_index.shape[0]
    width_aux = three_index.shape[1]
    pair_block = coeff.shape[0]
    width_pao = coeff.shape[1]
    width_virt = coeff.shape[2]
    slot_count = SLOTS
    pao_scale = 1.0 / math.sqrt(width_pao)
    aux_scale = 1.0 / math.sqrt(width_aux)
    virt_scale = 1.0 / math.sqrt(width_virt)
    occ_local = jnp.mod(pair_occ - (column - 1) * occ_block, occ_block * column_count)
    partner_local = jnp.mod(partners - (column - 1) * pair_block, pair_block * column_count)
    positions = jnp.arange(pair_block, dtype=jnp.int32)
    same_owner = (pair_owner[:, None] == pair_owner[None, :]).astype(jnp.int32)
    earlier = (positions[None, :] < positions[:, None]).astype(jnp.int32)
    pair_ranks = jnp.sum(same_owner * earlier, axis=1)
    gathered_at = pair_owner * slot_count + pair_ranks
    owned_here = pair_owner == role_index
    slot_ids = jnp.arange(slot_count, dtype=jnp.int32)
    slot_hits = (owned_here[None, :] & (pair_ranks[None, :] == slot_ids[:, None])).astype(jnp.int32)
    slot_pair = jnp.sum(slot_hits * positions[None, :], axis=1)
    slot_valid = (jnp.sum(slot_hits, axis=1) > 0).astype(jnp.float32)
    virtuals = jnp.arange(width_virt, dtype=jnp.int32)
    blocks = extended(three_index, (("pairs", 0),), occ_block)

    def transform_rows(orbitals_all, first_ids, second_ids):

        def one_pair(packed):
            orbitals, first_at, second_at = packed
            first_half = (
                jnp.dot(blocks[first_at], orbitals, preferred_element_type=jnp.float32) * pao_scale
            ).astype(jnp.bfloat16)
            second_half = (
                jnp.dot(blocks[second_at], orbitals, preferred_element_type=jnp.float32) * pao_scale
            ).astype(jnp.bfloat16)
            return (
                jnp.einsum("qa,qb->ab", first_half, second_half, preferred_element_type=jnp.float32)
                * aux_scale
            )

        return lax.map(one_pair, (orbitals_all, first_ids, second_ids))

    def transform(orbitals_all):
        return transform_rows(orbitals_all, occ_local[:, 0], occ_local[:, 1])

    near_orbitals = extended(coeff, (("pairs", 0),), pair_block)

    def slot_intersections():

        def slot_one_slot(slot_at):
            pair_at = slot_pair[slot_at]
            partner_orb = near_orbitals[partner_local[pair_at]]
            return (
                jnp.einsum(
                    "mb,kmc->kbc", coeff[pair_at], partner_orb, preferred_element_type=jnp.float32
                )
                * (1.0 / width_pao)
            ).astype(jnp.bfloat16)

        return lax.map(slot_one_slot, slot_ids)

    intersections = lax.cond(
        role_index > 0,
        slot_intersections,
        lambda: jnp.zeros((slot_count, PARTNERS, width_virt, width_virt), jnp.bfloat16),
    )

    def refresh(slot_ints, amp_pairs, near_amps):

        def refresh_one_slot(slot_at):
            pair_at = slot_pair[slot_at]
            intersection = intersections[slot_at]
            partner_amp = near_amps[partner_local[pair_at]]
            middle = jnp.einsum(
                "kbc,kcd->kbd", intersection, partner_amp, preferred_element_type=jnp.float32
            ).astype(jnp.bfloat16)
            partner_terms = jnp.einsum(
                "kbd,ked->kbe", middle, intersection, preferred_element_type=jnp.float32
            )
            coupled = jnp.sum(coupling[pair_at][:, None, None] * partner_terms, axis=0)
            occ_shift = eps_occ[pair_occ[pair_at, 0]] + eps_occ[pair_occ[pair_at, 1]]
            energy = eps_virt[pair_at][:, None] + eps_virt[pair_at][None, :] - occ_shift
            own_amp = amp_pairs[pair_at].astype(jnp.float32)
            fresh_amp = own_amp - (
                slot_ints[slot_at].astype(jnp.float32) + energy * own_amp + coupled
            ) / (energy + 1.0)
            keep_rows = (virtuals < nvirt[pair_at]).astype(jnp.float32) * slot_valid[slot_at]
            fresh_amp = (fresh_amp * keep_rows[:, None] * keep_rows[None, :]).astype(jnp.bfloat16)
            dressed = (
                (
                    coeff[pair_at].astype(jnp.float32)
                    + jnp.dot(coeff[pair_at], fresh_amp, preferred_element_type=jnp.float32)
                    * virt_scale
                )
                * slot_valid[slot_at]
            ).astype(jnp.bfloat16)
            return (fresh_amp, dressed)

        return lax.map(refresh_one_slot, slot_ids)

    zero_amp = jnp.zeros((slot_count, width_virt, width_virt), jnp.bfloat16)
    zero_orb = jnp.zeros((slot_count, width_pao, width_virt), jnp.bfloat16)
    amp_pairs = amps
    orb_pairs = coeff
    slot_amps = zero_amp
    slot_orbs = jnp.take(coeff, slot_pair, axis=0)
    for iteration in range(ITERS):
        local_ints = lax.cond(
            role_index == 0,
            lambda: transform(orb_pairs).astype(jnp.bfloat16),
            lambda: jnp.zeros((pair_block, width_virt, width_virt), jnp.bfloat16),
        )
        pair_ints = from_root(local_ints, "role", 0)
        slot_ints = jnp.take(pair_ints, slot_pair, axis=0)
        near_amps = extended(amp_pairs, (("pairs", 0),), pair_block)
        slot_amps, slot_orbs = lax.cond(
            role_index > 0,
            lambda: refresh(slot_ints, amp_pairs, near_amps),
            lambda: (zero_amp, zero_orb),
        )
        if iteration + 1 < ITERS:
            every_amp, every_orb = (
                lax.all_gather(slot_amps, "role", axis=0, tiled=True),
                lax.all_gather(slot_orbs, "role", axis=0, tiled=True),
            )
            amp_pairs = jnp.take(every_amp, gathered_at, axis=0)
            orb_pairs = jnp.take(every_orb, gathered_at, axis=0)
    return (slot_amps, slot_orbs)


def solution(mesh):
    in_specs = (
        P("pairs", None, None),
        P("pairs", None, None),
        P("pairs", None, None),
        P("pairs", None),
        P(),
        P("pairs"),
        P("pairs", None),
        P("pairs", None),
        P("pairs", None),
        P("pairs"),
    )
    out_specs = (P(("role", "pairs"), None, None), P(("role", "pairs"), None, None))
    return jax.shard_map(local, mesh=mesh, in_specs=in_specs, out_specs=out_specs, check_vma=False)
```

profile of v0, /device:TPU:20, one launch (start us, length us, event | category | flops | bytes accessed | tf_op | source)
XLA Modules:
  0.0 408.2 jit_solution(528838157583865312)
XLA Ops:
  7.2 1.9 collective-permute-start
  9.1 10.8 %collective-permute-start.1 = (bf16[2,1024,512]{2,1,0:T(8,128)(2,1)}, bf16[2,1024,512]{2,1,0:T(8,128)(2,1)S(1)}, u32[]{:S(2)}, u32[]{:S(2)}) collective-permute-start(bf16[2,1024,512]{2,1,0:T(8,128)(2,1)} %param.32), channel_id=1, source_target_pairs={{1,0},{2,1},{3,2},{4,3},{5,4},{6,5},{7,6},{8,7},{9,8},{10,9},{11,1... | collective-permute-start | bytes 6291464 | tf_op jit(solution)/shard_map/ppermute | solution.py:22
  20.0 1.9 collective-permute-start.2
  21.9 5.8 %collective-permute-start.3 = (bf16[4,512,256]{2,1,0:T(8,128)(2,1)}, bf16[4,512,256]{2,1,0:T(8,128)(2,1)}, u32[]{:S(2)}, u32[]{:S(2)}) collective-permute-start(bf16[4,512,256]{2,1,0:T(8,128)(2,1)} %param.33), channel_id=1, source_target_pairs={{1,0},{2,1},{3,2},{4,3},{5,4},{6,5},{7,6},{8,7},{9,8},{10,9},{11,1... | collective-permute-start | bytes 3145736 | tf_op jit(solution)/shard_map/ppermute | solution.py:22
  27.7 1.9 collective-permute-start.4
  29.6 0.9 select_reduce_fusion
  31.3 0.7 and_select_fusion
  32.0 0.7 add_select_fusion
  32.7 9.3 %collective-permute-done = bf16[2,1024,512]{2,1,0:T(8,128)(2,1)} collective-permute-done((bf16[2,1024,512]{2,1,0:T(8,128)(2,1)}, bf16[2,1024,512]{2,1,0:T(8,128)(2,1)}, u32[]{:S(2)}, u32[]{:S(2)}) %collective-permute-start) | collective-permute-done | bytes 2097184 | tf_op jit(solution)/shard_map/ppermute | solution.py:20
  42.1 1.9 collective-permute-start.5
  44.0 3.0 constant_dynamic-update-slice_fusion.4
  47.0 1.5 constant_dynamic-update-slice_fusion.3
  48.6 1.5 constant_dynamic-update-slice_fusion.2
  50.2 0.8 conditional.5
  50.2 0.8 broadcast.416
  51.0 0.8 broadcast_select_fusion.5
  51.9 7.0 %collective-permute-done.4 = bf16[4,256,256]{2,1,0:T(8,128)(2,1)} collective-permute-done((bf16[4,256,256]{2,1,0:T(8,128)(2,1)}, bf16[4,256,256]{2,1,0:T(8,128)(2,1)}, u32[]{:S(2)}, u32[]{:S(2)}) %collective-permute-start.4) | collective-permute-done | bytes 524320 | tf_op jit(solution)/shard_map/ppermute | solution.py:20
  58.9 1.8 collective-permute-done.5
  60.7 2.5 pad_maximum_fusion.1
  63.2 2.0 pad_maximum_fusion
  65.3 20.9 %conditional.6 = (bf16[2,8,256,256]{2,3,1,0:T(8,128)(2,1)}) conditional(s32[]{:T(128)} %convert_element_type.100, () %tuple.66, (s32[2]{0:T(128)S(1)}, s32[2]{0:T(128)S(1)}, s32[4,8]{1,0:T(4,128)S(1)}, bf16[12,512,256]{2,1,0:T(8,128)(2,1)S(1)}, bf16[4,512,256]{2,1,0:T(8,128)(2,1)}) %tuple.67), branch_computations={%region_2.3_spmd, %region_3.6_spmd} | conditional | flops 537920512 | bytes 7607225 | solution.py:100
  65.4 20.9 %while.49 = (s32[]{:T(128)}, bf16[2,8,256,256]{2,3,1,0:T(8,128)(2,1)}, s32[2]{0:T(128)S(1)}, s32[2]{0:T(128)S(1)}, s32[4,8]{1,0:T(4,128)S(1)}, /*index=5*/bf16[1...) while((s32[]{:T(128)}, ...), condition=%wide.region_5.5_spmd, body=%wide.region_4.4_spmd.sunk | while | flops 537920512 | bytes 7607121 | solution.py:98
  70.4 2.0 gather_fusion.3
  72.5 3.3 fusion.176
  80.8 2.0 gather_fusion.3
  82.9 3.3 fusion.176
  86.2 56.5 %all-reduce.3.cloned.1.call-done = bf16[4,256,256]{2,1,0:T(8,128)(2,1)} async-done(((bf16[4,256,256]{2,1,0:T(8,128)(2,1)}), bf16[4,256,256]{2,1,0:T(8,128)(2,1)}) %all-reduce.3.cloned.1.call-update) | async-done | bytes 524304 | tf_op jit(solution)/shard_map/psum | solution.py:31
  142.7 1.6 gather_fusion.5
  144.4 42.6 %conditional.7 = (bf16[2,256,256]{2,1,0:T(8,128)(2,1)}, bf16[2,512,256]{2,1,0:T(8,128)(2,1)}) conditional(s32[]{:T(128)} %convert_element_type.100, () %tuple.63, (s32[2]{0:T(128)S(1)}, s32[2]{0:T(128)S(1)}, bf16[4,256,256]{2,1,0:T(8,128)(2,1)}, pred[2]{0:T(512)(128)(4,1)S(1)}, f32[4,256]{1,0:T(4,128)S(1)}, /*index=5*/s32[4,2]{0,1:T(2,128)S(1)}, ...), branch_computations={%region_12.14_spmd, %region_13.18_spmd} | conditional | flops 607127040 | bytes 12207015 | solution.py:154
  144.5 42.5 %while.52 = (s32[]{:T(128)}, bf16[2,256,256]{2,1,0:T(8,128)(2,1)}, bf16[2,512,256]{2,1,0:T(8,128)(2,1)}, s32[2]{0:T(128)S(1)}, s32[2]{0:T(128)S(1)}, /*index=5*/...) while((s32[]{:T(128)}, bf16[2,256,256]{2,1,0:T(8,128)(2,1)}, ...), condition=%wide.region_16.17_spmd, body=%wide.region_14.16_spmd.sunk | while | flops 606995968 | bytes 11420373 | solution.py:137
  149.5 2.0 gather_fusion.2
  151.5 2.4 multiply_reduce_fusion.5
  161.2 1.2 compare_select_fusion.13
  162.5 1.8 constant_dynamic-update-slice_fusion.8
  164.3 1.5 fusion.172
  170.7 2.0 gather_fusion.2
  172.8 2.4 multiply_reduce_fusion.5
  182.5 1.2 compare_select_fusion.13
  183.7 1.8 constant_dynamic-update-slice_fusion.8
  185.5 1.5 fusion.172
  187.1 0.7 all-gather.5.cloned.1.call-update
  187.8 31.6 %all-gather.3.cloned.1.call-done = bf16[8,256,256]{2,1,0:T(8,128)(2,1)} async-done(((bf16[2,256,256]{2,1,0:T(8,128)(2,1)}), bf16[8,256,256]{2,1,0:T(8,128)(2,1)}) %all-gather.3.cloned.1.call-update) | async-done | bytes 1048592 | tf_op jit(solution)/shard_map/all_gather | solution.py:161
  219.4 1.8 gather_fusion.4
  221.3 1.9 collective-permute-start.6
  223.3 5.8 %collective-permute-start.7 = (bf16[4,256,256]{2,1,0:T(8,128)(2,1)S(1)}, bf16[4,256,256]{2,1,0:T(8,128)(2,1)}, u32[]{:S(2)}, u32[]{:S(2)}) collective-permute-start(bf16[4,256,256]{2,1,0:T(8,128)(2,1)S(1)} %broadcast_select_fusion.3), channel_id=1, source_target_pairs={{1,0},{2,1},{3,2},{4,3},{5,4},{6,5},{7,6},{8,7},{9,8},{10,9},{11,1... | collective-permute-start | bytes 1572872 | tf_op jit(solution)/shard_map/ppermute | solution.py:22
  229.0 31.6 %all-gather.5.cloned.1.call-done = bf16[8,512,256]{2,1,0:T(8,128)(2,1)} async-done(((bf16[2,512,256]{2,1,0:T(8,128)(2,1)}), bf16[8,512,256]{2,1,0:T(8,128)(2,1)}) %all-gather.5.cloned.1.call-update) | async-done | bytes 2097168 | tf_op jit(solution)/shard_map/all_gather | solution.py:162
  260.7 0.8 conditional.8
  260.7 0.8 broadcast.432
  261.5 0.8 broadcast_select_fusion.4
  262.4 0.8 copy-done.4
  263.2 1.4 pad_maximum_fusion.2
  264.5 93.4 %all-reduce.5.cloned.1.call-done = bf16[4,256,256]{2,1,0:T(8,128)(2,1)} async-done(((bf16[4,256,256]{2,1,0:T(8,128)(2,1)}), bf16[4,256,256]{2,1,0:T(8,128)(2,1)}) %all-reduce.5.cloned.1.call-update) | async-done | bytes 524304 | tf_op jit(solution)/shard_map/psum | solution.py:31
  358.0 1.6 gather_fusion.6
  359.6 42.1 %conditional.9 = (bf16[2,256,256]{2,1,0:T(8,128)(2,1)}, bf16[2,512,256]{2,1,0:T(8,128)(2,1)}) conditional(s32[]{:T(128)} %convert_element_type.100, () %tuple.62, (s32[2]{0:T(128)S(1)}, s32[2]{0:T(128)S(1)}, bf16[4,256,256]{2,1,0:T(8,128)(2,1)S(1)}, pred[2]{0:T(512)(128)(4,1)S(1)}, f32[4,256]{1,0:T(4,128)S(1)}, /*index=5*/s32[4,2]{0,1:T(2,128)S(1)}, ...), branch_computations={%region_22.24_spmd, %region_23.28_spmd} | conditional | flops 607127040 | bytes 8012683 | solution.py:154
  359.6 0.8 broadcast_select_fusion.2
  360.4 41.3 %while.53 = (s32[]{:T(128)}, bf16[2,256,256]{2,1,0:T(8,128)(2,1)}, bf16[2,512,256]{2,1,0:T(8,128)(2,1)}, s32[2]{0:T(128)S(1)}, s32[2]{0:T(128)S(1)}, /*index=5*/...) while((s32[]{:T(128)}, bf16[2,256,256]{2,1,0:T(8,128)(2,1)}, ...), condition=%wide.region_26.27_spmd, body=%wide.region_24.26_spmd.sunk | while | flops 606995968 | bytes 7226041 | solution.py:137
  366.1 2.4 multiply_reduce_fusion.4
  375.6 1.2 compare_select_fusion.12
  376.8 1.8 constant_dynamic-update-slice_fusion.7
  378.6 2.5 fusion.156
  386.8 2.3 multiply_reduce_fusion.4
  396.2 1.2 compare_select_fusion.12
  397.4 1.8 constant_dynamic-update-slice_fusion.7
  399.2 2.5 fusion.156
  (102 shorter events, 19.9 us)
Async XLA Ops:
  7.2 135.5 %all-reduce.3.cloned.1.call-start = ((), (), s32[]{:S(2)}) async-start(), calls=%async_computation | async-start | bytes 1048576 | tf_op jit(solution)/shard_map/psum | solution.py:31
  7.2 34.8 %collective-permute-start = (bf16[2,1024,512]{2,1,0:T(8,128)(2,1)}, bf16[2,1024,512]{2,1,0:T(8,128)(2,1)}, u32[]{:S(2)}, u32[]{:S(2)}) collective-permute-start(bf16[2,1024,512]{2,1,0:T(8,128)(2,1)} %param.32), channel_id=1, source_target_pairs={{0,1},{1,2},{2,3},{3,4},{4,5},{5,6},{6,7},{7,8},{8,9},{9,10},{10,1... | collective-permute-start | bytes 6291464 | tf_op jit(solution)/shard_map/ppermute | solution.py:20
  9.1 39.4 %collective-permute-start.1 = (bf16[2,1024,512]{2,1,0:T(8,128)(2,1)}, bf16[2,1024,512]{2,1,0:T(8,128)(2,1)S(1)}, u32[]{:S(2)}, u32[]{:S(2)}) collective-permute-start(bf16[2,1024,512]{2,1,0:T(8,128)(2,1)} %param.32), channel_id=1, source_target_pairs={{1,0},{2,1},{3,2},{4,3},{5,4},{6,5},{7,6},{8,7},{9,8},{10,9},{11,1... | collective-permute-start | bytes 6291464 | tf_op jit(solution)/shard_map/ppermute | solution.py:22
  20.0 43.2 %collective-permute-start.2 = (bf16[4,512,256]{2,1,0:T(8,128)(2,1)}, bf16[4,512,256]{2,1,0:T(8,128)(2,1)}, u32[]{:S(2)}, u32[]{:S(2)}) collective-permute-start(bf16[4,512,256]{2,1,0:T(8,128)(2,1)} %param.33), channel_id=1, source_target_pairs={{0,1},{1,2},{2,3},{3,4},{4,5},{5,6},{6,7},{7,8},{8,9},{9,10},{10,1... | collective-permute-start | bytes 3145736 | tf_op jit(solution)/shard_map/ppermute | solution.py:20
  21.9 41.3 %collective-permute-start.3 = (bf16[4,512,256]{2,1,0:T(8,128)(2,1)}, bf16[4,512,256]{2,1,0:T(8,128)(2,1)}, u32[]{:S(2)}, u32[]{:S(2)}) collective-permute-start(bf16[4,512,256]{2,1,0:T(8,128)(2,1)} %param.33), channel_id=1, source_target_pairs={{1,0},{2,1},{3,2},{4,3},{5,4},{6,5},{7,6},{8,7},{9,8},{10,9},{11,1... | collective-permute-start | bytes 3145736 | tf_op jit(solution)/shard_map/ppermute | solution.py:22
  27.7 31.2 %collective-permute-start.4 = (bf16[4,256,256]{2,1,0:T(8,128)(2,1)}, bf16[4,256,256]{2,1,0:T(8,128)(2,1)}, u32[]{:S(2)}, u32[]{:S(2)}) collective-permute-start(bf16[4,256,256]{2,1,0:T(8,128)(2,1)} %param.34), channel_id=1, source_target_pairs={{0,1},{1,2},{2,3},{3,4},{4,5},{5,6},{6,7},{7,8},{8,9},{9,10},{10,1... | collective-permute-start | bytes 1572872 | tf_op jit(solution)/shard_map/ppermute | solution.py:20
  32.7 14.3 %copy-start.1 = (bf16[2,1024,512]{2,1,0:T(8,128)(2,1)S(1)}, bf16[2,1024,512]{2,1,0:T(8,128)(2,1)}, u32[]{:S(2)}) copy-start(bf16[2,1024,512]{2,1,0:T(8,128)(2,1)} %param.32) | copy-start | bytes 6291460
  42.1 18.6 %collective-permute-start.5 = (bf16[4,256,256]{2,1,0:T(8,128)(2,1)}, bf16[4,256,256]{2,1,0:T(8,128)(2,1)}, u32[]{:S(2)}, u32[]{:S(2)}) collective-permute-start(bf16[4,256,256]{2,1,0:T(8,128)(2,1)} %param.34), channel_id=1, source_target_pairs={{1,0},{2,1},{3,2},{4,3},{5,4},{6,5},{7,6},{8,7},{9,8},{10,9},{11,1... | collective-permute-start | bytes 1572872 | tf_op jit(solution)/shard_map/ppermute | solution.py:22
  48.5 1.6 copy-start.2
  50.2 10.5 %copy-start = (bf16[4,256,256]{2,1,0:T(8,128)(2,1)S(1)}, bf16[4,256,256]{2,1,0:T(8,128)(2,1)}, u32[]{:S(2)}) copy-start(bf16[4,256,256]{2,1,0:T(8,128)(2,1)} %param.34) | copy-start | bytes 1572868
  51.9 167.5 %all-gather.3.cloned.1.call-start = ((), (), s32[]{:S(2)}) async-start(), calls=%async_computation.1 | async-start | bytes 1310720 | tf_op jit(solution)/shard_map/all_gather | solution.py:161
  65.3 79.1 %copy-start.5 = (s32[4,2]{0,1:T(2,128)S(1)}, s32[4,2]{0,1:T(2,128)}, u32[]{:S(2)}) copy-start(s32[4,2]{0,1:T(2,128)} %param.38) | copy-start | bytes 100
  65.3 79.1 %copy-start.6 = (f32[256]{0:T(256)S(1)}, f32[256]{0:T(256)}, u32[]{:S(2)}) copy-start(f32[256]{0:T(256)} %param.36) | copy-start | bytes 3076
  65.3 79.1 %copy-start.7 = (f32[4,256]{1,0:T(4,128)S(1)}, f32[4,256]{1,0:T(4,128)}, u32[]{:S(2)}) copy-start(f32[4,256]{1,0:T(4,128)} %param.35) | copy-start | bytes 12292
  65.3 79.1 %copy-start.8 = (f32[4,8]{1,0:T(4,128)S(1)}, f32[4,8]{1,0:T(4,128)}, u32[]{:S(2)}) copy-start(f32[4,8]{1,0:T(4,128)} %param.40) | copy-start | bytes 388
  65.3 79.1 %copy-start.9 = (s32[4]{0:T(128)S(1)}, s32[4]{0:T(128)}, u32[]{:S(2)}) copy-start(s32[4]{0:T(128)} %param.37) | copy-start | bytes 52
  151.5 12.8 %copy-start.3 = (bf16[4,512,256]{2,1,0:T(8,128)(2,1)S(1)}, bf16[4,512,256]{2,1,0:T(8,128)(2,1)}, u32[]{:S(2)}) copy-start(bf16[4,512,256]{2,1,0:T(8,128)(2,1)} %get-tuple-element.1188) | copy-start | bytes 3145732 | tf_op jit(solution)/shard_map/cond/branch_1_fun/while
  172.7 12.8 %copy-start.3 = (bf16[4,512,256]{2,1,0:T(8,128)(2,1)S(1)}, bf16[4,512,256]{2,1,0:T(8,128)(2,1)}, u32[]{:S(2)}) copy-start(bf16[4,512,256]{2,1,0:T(8,128)(2,1)} %get-tuple-element.1188) | copy-start | bytes 3145732 | tf_op jit(solution)/shard_map/cond/branch_1_fun/while
  187.0 73.6 %all-gather.5.cloned.1.call-start = ((), (), s32[]{:S(2)}) async-start(), calls=%async_computation.2 | async-start | bytes 2621440 | tf_op jit(solution)/shard_map/all_gather | solution.py:162
  187.8 170.2 %all-reduce.5.cloned.1.call-start = ((), (), s32[]{:S(2)}) async-start(), calls=%async_computation.3 | async-start | bytes 1048576 | tf_op jit(solution)/shard_map/psum | solution.py:31
  221.3 41.0 %collective-permute-start.6 = (bf16[4,256,256]{2,1,0:T(8,128)(2,1)S(1)}, bf16[4,256,256]{2,1,0:T(8,128)(2,1)S(1)}, u32[]{:S(2)}, u32[]{:S(2)}) collective-permute-start(bf16[4,256,256]{2,1,0:T(8,128)(2,1)S(1)} %broadcast_select_fusion.3), channel_id=1, source_target_pairs={{0,1},{1,2},{2,3},{3,4},{4,5},{5,6},{6,7},{7,8},{8,9},{9,10},{10,1... | collective-permute-start | bytes 1572872 | tf_op jit(solution)/shard_map/ppermute | solution.py:20
  223.3 39.9 %collective-permute-start.7 = (bf16[4,256,256]{2,1,0:T(8,128)(2,1)S(1)}, bf16[4,256,256]{2,1,0:T(8,128)(2,1)}, u32[]{:S(2)}, u32[]{:S(2)}) collective-permute-start(bf16[4,256,256]{2,1,0:T(8,128)(2,1)S(1)} %broadcast_select_fusion.3), channel_id=1, source_target_pairs={{1,0},{2,1},{3,2},{4,3},{5,4},{6,5},{7,6},{8,7},{9,8},{10,9},{11,1... | collective-permute-start | bytes 1572872 | tf_op jit(solution)/shard_map/ppermute | solution.py:22
  262.4 0.8 copy-start.4
Sparse Core Ops, SparseCore 0:
  52.0 90.6 all-reduce.2
  187.2 32.2 all-gather.2
  222.1 38.5 all-gather.4
  262.9 95.0 all-reduce.4
where the time goes:
time: 410 us; the launch traced here: 408 us
  waiting for transfers between devices  232 us (57%)
  loops' own time  42 us (10%)
  local copies, waits for them, and re-layouts  40.2 us (10%)
  starting transfers between devices  32.1 us (8%)
  matrix products  24.2 us (6%)
  other arithmetic  23.8 us (6%)
  between operations  14.1 us (3%)
    psum x2, waiting for transfers between devices, from_root(): return lax.psum(kept, axis)  150 us
    another operation x2, loops' own time, refresh(): return lax.map(refresh_one_slot, slot_ids)  34.3 us
    all_gather x1, waiting for transfers between devices, local(): lax.all_gather(slot_orbs, 'role', axis=0, tiled=True)  31.6 us
    all_gather x1, waiting for transfers between devices, local(): lax.all_gather(slot_amps, 'role', axis=0, tiled=True)  31.6 us
    ppermute x4, starting transfers between devices, extended(): lax.ppermute(head, axis, [((i + 1) % count, i) for i in range(count)])  24.2 us
    ppermute x4, waiting for transfers between devices, extended(): lax.ppermute(tail, axis, [(i, (i + 1) % count) for i in range(count)])  16.3 us
    dot_general x4, matrix products, refresh_one_slot(): jnp.einsum('kbd,ked->kbe', middle, intersection, preferred_element_type=j...  9.54 us
  transfers between devices with their start and end apart: 12, of which 7 were waited for; matrix products, arithmetic and copies ran while one was open for 8% of the time, Pallas kernels for 0%

commit v1 on v0

v1 whole, which is shorter than its diff:
```python
import functools
import math

import jax
import jax.numpy as jnp
from jax import lax
from jax.experimental import pallas as pl
from jax.experimental.pallas import tpu as pltpu
from jax.sharding import PartitionSpec as P

SLOTS = 2
MESH = pl.DeviceIdType.MESH
BF = jnp.bfloat16
F32 = jnp.float32

OCC, PART, COUP, XM, YM, CM, T1D, T1F, C2M, T2D, T2F, COUNT = 0, 2, 4, 6, 10, 14, 16, 20, 24, 28, 32, 36


def dot(a, b):
    return jnp.dot(a, b, preferred_element_type=F32)


def dot_nt(a, b):
    return lax.dot_general(a, b, (((1,), (1,)), ((), ())), preferred_element_type=F32)


def kernel(
    n, roles,
    three_hbm, coeff_hbm, amps_hbm, occ_hbm, part_hbm, coup_hbm,
    ev_ref, eo_ref, nv_ref, occ_ref, part_ref, coup_ref, own_ref,
    out_amp, out_orb,
    b_v, a_v, t_v, x_in, y_out, y_left, y_right, yit_v, s_v, u_v, c_out, c_in, c_own, rm_v, k_v,
    t1_v, t1_f, c2_out, c2_in, t2_v,
    occ_in, part_in, coup_in,
    load_sem, send_sem, recv_sem,
):
    r = lax.axis_index("role")
    c = lax.axis_index("pairs")
    up, down = lax.rem(r + 1, roles), lax.rem(r + roles - 1, roles)
    naux, npao = b_v.shape[1], b_v.shape[2]
    nv = a_v.shape[2]
    hw = nv // 2
    hr = nv // 2
    pao_scale = 1.0 / math.sqrt(npao)
    aux_scale = 1.0 / math.sqrt(naux)
    virt_scale = 1.0 / math.sqrt(nv)
    y_in = (y_left, y_right)
    near = lax.rem(c, 2)

    def remote(src, dst, base, s_at, r_at, device):
        return pltpu.make_async_remote_copy(
            src_ref=src, dst_ref=dst,
            send_sem=send_sem.at[base + s_at], recv_sem=recv_sem.at[base + r_at],
            device_id=device, device_id_type=MESH,
        )

    def side(d):
        return (r, lax.rem(c + 2 * d - 1 + n, n))

    def level(v):
        return (lax.rem(r + 1 + 2 * v, roles), c)

    def meta(d):
        return (
            remote(occ_hbm, occ_in.at[1 - d], OCC, d, 1 - d, side(d)),
            remote(part_hbm, part_in.at[1 - d], PART, d, 1 - d, side(d)),
            remote(coup_hbm, coup_in.at[1 - d], COUP, d, 1 - d, side(d)),
        )

    def xmsg(d, h):
        cols = pl.ds(h * hw, hw)
        return remote(coeff_hbm.at[r, :, cols], x_in.at[1 - d, :, cols], XM, 2 * d + h, 2 * (1 - d) + h, side(d))

    def ymsg(d, h):
        return remote(y_out.at[d, h], y_in[h].at[2 * (1 - d)], YM, 2 * d + h, 2 * (1 - d) + h, side(d))

    def cmsg(d):
        return remote(c_out.at[d], c_in.at[1 - d], CM, d, 1 - d, side(d))

    def c2msg(d, h):
        return remote(c2_out.at[d, h], c2_in.at[1 - d, h], C2M, 2 * d + h, 2 * (1 - d) + h, side(d))

    def direct(buf, base, v, h):
        return remote(buf.at[r, h], buf.at[r, h], base, 2 * v + h, 2 * (1 - v) + h, level(v))

    def forward(buf, base, v, h):
        which = down if v == 0 else up
        part = buf.at[which, h, pl.ds(v * hr, hr)]
        return remote(part, part, base, 2 * v + h, 2 * (1 - v) + h, level(v))

    load_a = pltpu.make_async_copy(coeff_hbm, a_v, load_sem.at[0])
    load_b = pltpu.make_async_copy(three_hbm, b_v, load_sem.at[1])
    load_t = pltpu.make_async_copy(amps_hbm, t_v, load_sem.at[2])
    load_a.start()
    load_b.start()
    load_t.start()

    barrier = pltpu.get_barrier_semaphore()
    for device in (side(0), side(1), level(0), level(1)):
        pl.semaphore_signal(barrier, inc=1, device_id=device, device_id_type=MESH)
    pl.semaphore_wait(barrier, 4)

    order = (near, 1 - near)
    for d in order:
        for message in meta(d):
            message.start()
    for h in range(2):
        for d in order:
            xmsg(d, h).start()

    second = lax.rem(occ_ref[r, 1] - 2 * (c - 1) + 2 * n, 2 * n)
    where_j = jnp.minimum(second // 2, 2)
    i_at = lax.rem(occ_ref[r, 0], 2)
    j_at = lax.rem(occ_ref[r, 1], 2)
    occ_shift = eo_ref[occ_ref[r, 0]] + eo_ref[occ_ref[r, 1]]
    count = nv_ref[r]

    def weights(parts, coups):
        out = []
        for q in range(roles):
            total = jnp.float32(0.0)
            for k in range(part_ref.shape[1]):
                total = total + jnp.where(parts(k) == roles * c + q, coups(k), jnp.float32(0.0))
            out.append(total)
        return out

    def overlap(x, at):
        xt = x.T
        for q in range(roles):
            s_v[at, :, q * nv:(q + 1) * nv] = (dot(xt, a_v[q]) * (1.0 / npao)).astype(BF)

    def coupled(at, w, amp):
        for q in range(roles):
            u_v[:, q * nv:(q + 1) * nv] = (dot(s_v[at, :, q * nv:(q + 1) * nv], amp(q)) * w[q]).astype(BF)
        return dot_nt(u_v[...], s_v[at])

    rows = lax.broadcasted_iota(jnp.int32, (nv, nv), 0)
    cols = lax.broadcasted_iota(jnp.int32, (nv, nv), 1)
    ev = jnp.broadcast_to(ev_ref[pl.ds(r, 1), :], (nv, nv))
    keep = (rows < count) & (cols < count)
    rm_v[...] = jnp.where(keep, 1.0 / (ev + ev.T - occ_shift + 1.0), 0.0)
    w_own = weights(lambda k: part_ref[r, k], lambda k: coup_ref[r, k])

    load_a.wait()
    load_b.wait()
    own = a_v[r]
    yit_v[...] = (dot(b_v[i_at], own) * pao_scale).astype(BF).T
    yj = (dot(b_v[j_at], own) * pao_scale).astype(BF)
    for h in range(2):
        y_in[h][1] = yj[:, h * hw:(h + 1) * hw]
    load_t.wait()
    overlap(own, 2)
    c_own[...] = coupled(2, w_own, lambda q: t_v[q])

    for h in range(2):
        for d in order:
            if h == 0:
                for message in meta(1 - d):
                    message.wait_recv()
            xmsg(1 - d, h).wait_recv()
            j_near = lax.rem(occ_in[d, r, 1], 2)
            y_out[d, h] = (dot(b_v[j_near], x_in[d, :, h * hw:(h + 1) * hw]) * pao_scale).astype(BF)
            if h == 0:
                ymsg(d, h).start()
    w_near = []
    for d in order:
        w = weights(lambda k: part_in[d, r, k], lambda k: coup_in[d, r, k])
        w_near.append(w)
        overlap(x_in[d], d)
        c_out[d] = coupled(d, w, lambda q: t_v[q]).astype(BF)
        cmsg(d).start()
        ymsg(d, 1).start()

    for d in range(2):
        cmsg(d).wait_recv()
    for h in range(2):
        for d in range(2):
            ymsg(d, h).wait_recv()
        lanes = slice(h * hw, (h + 1) * hw)
        k1 = dot(yit_v[...], y_in[h][where_j]) * aux_scale
        k_v[:, lanes] = k1
        total = k1 + c_own[:, lanes] + c_in[0, :, lanes].astype(F32) + c_in[1, :, lanes].astype(F32)
        fresh = rm_v[:, lanes] * (t_v[r, :, lanes].astype(F32) - total)
        t1_v[r, h] = fresh.astype(BF)
        for v in range(2):
            direct(t1_v, T1D, v, h).start()
        t1_f[:, lanes] = fresh

    def whole(buf, at):
        return jnp.concatenate([buf[at, 0], buf[at, 1]], axis=1)

    t1 = t1_f[...].astype(BF)
    half = k_v[...] + dot(k_v[...].astype(BF), t1) * virt_scale
    k2 = half + dot(t1.T, half.astype(BF)) * virt_scale
    k_v[...] = t1_f[...] - k2

    for h in range(2):
        for v in range(2):
            direct(t1_v, T1D, 1 - v, h).wait_recv()
            forward(t1_v, T1F, 1 - v, h).start()
    for h in range(2):
        for v in range(2):
            forward(t1_v, T1F, v, h).wait_recv()

    for at, d in enumerate(order):
        part = coupled(d, w_near[at], lambda q: whole(t1_v, q)).astype(BF)
        for h in range(2):
            c2_out[d, h] = part[:, h * hw:(h + 1) * hw]
            c2msg(d, h).start()
    k_v[...] = k_v[...] - coupled(2, w_own, lambda q: whole(t1_v, q))

    for h in range(2):
        for d in range(2):
            c2msg(d, h).wait_recv()
        lanes = slice(h * hw, (h + 1) * hw)
        total = k_v[:, lanes] - c2_in[0, h].astype(F32) - c2_in[1, h].astype(F32)
        t2_v[r, h] = (rm_v[:, lanes] * total).astype(BF)
        for v in range(2):
            direct(t2_v, T2D, v, h).start()

    slots = []
    for s in range(SLOTS):
        pair, found = jnp.int32(0), jnp.int32(0)
        for q in range(roles):
            rank = jnp.int32(0)
            for e in range(q):
                rank = rank + jnp.where(own_ref[e] == own_ref[q], 1, 0)
            hit = jnp.where((own_ref[q] == r) & (rank == s), 1, 0)
            pair = pair + q * hit
            found = found + hit
        slots.append((pair, found.astype(F32)))

    for h in range(2):
        for v in range(2):
            direct(t2_v, T2D, 1 - v, h).wait_recv()
            forward(t2_v, T2F, 1 - v, h).start()
    for h in range(2):
        for v in range(2):
            forward(t2_v, T2F, v, h).wait_recv()
    for s, (pair, found) in enumerate(slots):
        amp = whole(t2_v, pair)
        out_amp[s] = (amp.astype(F32) * found).astype(BF)
        orb = a_v[pair]
        out_orb[s] = ((orb.astype(F32) + dot(orb, amp) * virt_scale) * found).astype(BF)

    for d in range(2):
        for message in meta(d):
            message.wait_send()
        cmsg(d).wait_send()
        for h in range(2):
            xmsg(d, h).wait_send()
            ymsg(d, h).wait_send()
            c2msg(d, h).wait_send()
            for buf, base, again in ((t1_v, T1D, T1F), (t2_v, T2D, T2F)):
                direct(buf, base, d, h).wait_send()
                forward(buf, again, d, h).wait_send()


def local(three_index, coeff, amps, eps_virt, eps_occ, nvirt, pair_occ, partners, coupling, pair_owner):
    n, roles = lax.axis_size("pairs"), lax.axis_size("role")
    _, naux, npao = three_index.shape
    pairs, _, nv = coeff.shape
    anywhere = pl.BlockSpec(memory_space=pl.ANY)
    scalars = pl.BlockSpec(memory_space=pltpu.SMEM)
    vector = pl.BlockSpec(memory_space=pltpu.VMEM)
    hw = nv // 2
    return pl.pallas_call(
        functools.partial(kernel, n, roles),
        out_shape=(
            jax.ShapeDtypeStruct((SLOTS, nv, nv), BF),
            jax.ShapeDtypeStruct((SLOTS, npao, nv), BF),
        ),
        in_specs=[anywhere] * 6 + [vector] + [scalars] * 6,
        out_specs=(vector, vector),
        scratch_shapes=[
            pltpu.VMEM(three_index.shape, BF),
            pltpu.VMEM(coeff.shape, BF),
            pltpu.VMEM(amps.shape, BF),
            pltpu.VMEM((2, npao, nv), BF),
            pltpu.VMEM((2, 2, naux, hw), BF),
            pltpu.VMEM((3, naux, hw), BF),
            pltpu.VMEM((3, naux, hw), BF),
            pltpu.VMEM((nv, naux), BF),
            pltpu.VMEM((3, nv, pairs * nv), BF),
            pltpu.VMEM((nv, pairs * nv), BF),
            pltpu.VMEM((2, nv, nv), BF),
            pltpu.VMEM((2, nv, nv), BF),
            pltpu.VMEM((nv, nv), F32),
            pltpu.VMEM((nv, nv), F32),
            pltpu.VMEM((nv, nv), F32),
            pltpu.VMEM((pairs, 2, nv, hw), BF),
            pltpu.VMEM((nv, nv), F32),
            pltpu.VMEM((2, 2, nv, hw), BF),
            pltpu.VMEM((2, 2, nv, hw), BF),
            pltpu.VMEM((pairs, 2, nv, hw), BF),
            pltpu.SMEM((2,) + pair_occ.shape, jnp.int32),
            pltpu.SMEM((2,) + partners.shape, jnp.int32),
            pltpu.SMEM((2,) + coupling.shape, F32),
            pltpu.SemaphoreType.DMA((3,)),
            pltpu.SemaphoreType.DMA((COUNT,)),
            pltpu.SemaphoreType.DMA((COUNT,)),
        ],
        compiler_params=pltpu.CompilerParams(
            collective_id=0, has_side_effects=True, vmem_limit_bytes=48 * 1024 * 1024
        ),
    )(
        three_index, coeff, amps, pair_occ, partners, coupling,
        eps_virt, eps_occ, nvirt, pair_occ, partners, coupling, pair_owner,
    )


def solution(mesh):
    in_specs = (
        P("pairs", None, None),
        P("pairs", None, None),
        P("pairs", None, None),
        P("pairs", None),
        P(),
        P("pairs"),
        P("pairs", None),
        P("pairs", None),
        P("pairs", None),
        P("pairs"),
    )
    out_specs = (P(("role", "pairs"), None, None), P(("role", "pairs"), None, None))
    return jax.shard_map(local, mesh=mesh, in_specs=in_specs, out_specs=out_specs, check_vma=False)
```

time: 410 us -> 60.1 us (0.15)
  the two profiles are of different devices: /device:TPU:20 before, /device:TPU:16 now
where the time goes in v1:
time: 60.1 us; the launch traced here: 59.7 us
  Pallas kernels  48.9 us (81%)
  local copies, waits for them, and re-layouts  10.2 us (17%)
  between operations  0.65 us (1%)
    pallas_call x1, Pallas kernels, local(): pl.pallas_call(functools.partial(kernel, n, roles), out_shape=(jax.ShapeD...  48.9 us
    unnamed x21, local copies, waits for them, and re-layouts  10.2 us

profile of v1, /device:TPU:16, one launch (start us, length us, event | category | flops | bytes accessed | tf_op | source)
XLA Modules:
  0.0 59.7 jit_solution(4549061763300195161)
XLA Ops:
  0.6 0.8 %copy.12.occ_hbm.occ_ref = s32[4,2]{1,0:T(4,128)S(1)} copy(s32[4,2]{0,1:T(2,128)} %param.16) | data formatting | bytes 64 | tf_op args[6]
  1.4 0.0 copy-start
  1.4 1.6 %copy-done = bf16[2,1024,512]{2,1,0:T(8,128)(2,1)S(1)} copy-done((bf16[2,1024,512]{2,1,0:T(8,128)(2,1)S(1)}, bf16[2,1024,512]{2,1,0:T(8,128)(2,1)}, u32[]{:S(2)}) %copy-start) | copy-done | bytes 2097176
  3.0 0.0 copy-start.1
  3.0 1.2 %copy-done.1 = bf16[4,512,256]{2,1,0:T(8,128)(2,1)S(1)} copy-done((bf16[4,512,256]{2,1,0:T(8,128)(2,1)S(1)}, bf16[4,512,256]{2,1,0:T(8,128)(2,1)}, u32[]{:S(2)}) %copy-start.1) | copy-done | bytes 1048600
  4.2 0.0 copy-start.2
  4.2 1.0 %copy-done.2 = bf16[4,256,256]{2,1,0:T(8,128)(2,1)S(1)} copy-done((bf16[4,256,256]{2,1,0:T(8,128)(2,1)S(1)}, bf16[4,256,256]{2,1,0:T(8,128)(2,1)}, u32[]{:S(2)}) %copy-start.2) | copy-done | bytes 524312
  5.3 0.0 copy-start.3
  5.3 0.7 %copy-done.3 = s32[4,8]{1,0:T(4,128)S(1)} copy-done((s32[4,8]{1,0:T(4,128)S(1)}, s32[4,8]{1,0:T(4,128)}, u32[]{:S(2)}) %copy-start.3) | copy-done | bytes 152
  5.9 0.0 copy-start.4
  5.9 0.7 %copy-done.4 = f32[4,8]{1,0:T(4,128)S(1)} copy-done((f32[4,8]{1,0:T(4,128)S(1)}, f32[4,8]{1,0:T(4,128)}, u32[]{:S(2)}) %copy-start.4) | copy-done | bytes 152
  6.6 0.0 copy-start.5
  6.6 0.7 %copy-done.5 = f32[4,256]{1,0:T(4,128)S(1)} copy-done((f32[4,256]{1,0:T(4,128)S(1)}, f32[4,256]{1,0:T(4,128)}, u32[]{:S(2)}) %copy-start.5) | copy-done | bytes 4120
  7.3 0.0 copy-start.6
  7.3 0.7 %copy-done.6 = f32[256]{0:T(256)S(1)} copy-done((f32[256]{0:T(256)S(1)}, f32[256]{0:T(256)}, u32[]{:S(2)}) %copy-start.6) | copy-done | bytes 1048
  8.0 0.0 copy-start.7
  8.0 0.7 %copy-done.7 = s32[4]{0:T(128)S(1)} copy-done((s32[4]{0:T(128)S(1)}, s32[4]{0:T(128)}, u32[]{:S(2)}) %copy-start.7) | copy-done | bytes 40
  8.6 0.0 copy-start.8
  8.6 0.7 %copy-done.8 = s32[4]{0:T(128)S(1)} copy-done((s32[4]{0:T(128)S(1)}, s32[4]{0:T(128)}, u32[]{:S(2)}) %copy-start.8) | copy-done | bytes 40
  9.3 48.9 %shard_map.113 = (bf16[2,256,256]{2,1,0:T(8,128)(2,1)S(1)}, bf16[2,512,256]{2,1,0:T(8,128)(2,1)S(1)}) custom-call(bf16[2,1024,512]{2,1,0:T(8,128)(2,1)S(1)} %copy-done, bf16[4,512,256]{2,1,0:T(8,128)(2,1)S(1)} %copy-done.1, bf16[4,256,256]{2,1,0:T(8,128)(2,1)S(1)} %copy-done.2, s32[4,2]{1,0:T(4,128)S(1)} %copy.12.occ_hbm.occ_ref, s32[4,8]{1,0:T(4,128)S(1)} %copy-done.3, ...), custom_call_target="tpu_custom_call" | custom-call | tf_op jit(solution)/shard_map/pallas_call | solution.py:267
  58.2 0.7 %copy.16 = bf16[2,256,256]{2,1,0:T(8,128)(2,1)} copy(bf16[2,256,256]{2,1,0:T(8,128)(2,1)S(1)} %get-tuple-element.4) | data formatting | bytes 524288
  58.9 0.8 %copy.17 = bf16[2,512,256]{2,1,0:T(8,128)(2,1)} copy(bf16[2,512,256]{2,1,0:T(8,128)(2,1)S(1)} %get-tuple-element.5) | data formatting | bytes 1048576
Async XLA Ops:
  1.4 1.6 %copy-start = (bf16[2,1024,512]{2,1,0:T(8,128)(2,1)S(1)}, bf16[2,1024,512]{2,1,0:T(8,128)(2,1)}, u32[]{:S(2)}) copy-start(bf16[2,1024,512]{2,1,0:T(8,128)(2,1)} %three_hbm.1) | copy-start | bytes 6291460
  3.0 1.2 %copy-start.1 = (bf16[4,512,256]{2,1,0:T(8,128)(2,1)S(1)}, bf16[4,512,256]{2,1,0:T(8,128)(2,1)}, u32[]{:S(2)}) copy-start(bf16[4,512,256]{2,1,0:T(8,128)(2,1)} %coeff_hbm.1) | copy-start | bytes 3145732
  4.2 1.0 %copy-start.2 = (bf16[4,256,256]{2,1,0:T(8,128)(2,1)S(1)}, bf16[4,256,256]{2,1,0:T(8,128)(2,1)}, u32[]{:S(2)}) copy-start(bf16[4,256,256]{2,1,0:T(8,128)(2,1)} %amps_hbm.1) | copy-start | bytes 1572868
  5.3 0.7 %copy-start.3 = (s32[4,8]{1,0:T(4,128)S(1)}, s32[4,8]{1,0:T(4,128)}, u32[]{:S(2)}) copy-start(s32[4,8]{1,0:T(4,128)} %part_ref.1) | copy-start | bytes 388
  5.9 0.7 %copy-start.4 = (f32[4,8]{1,0:T(4,128)S(1)}, f32[4,8]{1,0:T(4,128)}, u32[]{:S(2)}) copy-start(f32[4,8]{1,0:T(4,128)} %coup_ref.1) | copy-start | bytes 388
  6.6 0.7 %copy-start.5 = (f32[4,256]{1,0:T(4,128)S(1)}, f32[4,256]{1,0:T(4,128)}, u32[]{:S(2)}) copy-start(f32[4,256]{1,0:T(4,128)} %ev_ref.1) | copy-start | bytes 12292
  7.3 0.7 %copy-start.6 = (f32[256]{0:T(256)S(1)}, f32[256]{0:T(256)}, u32[]{:S(2)}) copy-start(f32[256]{0:T(256)} %eo_ref.1) | copy-start | bytes 3076
  8.0 0.7 %copy-start.7 = (s32[4]{0:T(128)S(1)}, s32[4]{0:T(128)}, u32[]{:S(2)}) copy-start(s32[4]{0:T(128)} %nv_ref.1) | copy-start | bytes 52
  8.6 0.7 %copy-start.8 = (s32[4]{0:T(128)S(1)}, s32[4]{0:T(128)}, u32[]{:S(2)}) copy-start(s32[4]{0:T(128)} %own_ref.1) | copy-start | bytes 52

commit v2 on v1

v2 whole, which is shorter than its diff:
```python
import functools
import math

import jax
import jax.numpy as jnp
from jax import lax
from jax.experimental import pallas as pl
from jax.experimental.pallas import tpu as pltpu
from jax.sharding import PartitionSpec as P

SLOTS = 2
MESH = pl.DeviceIdType.MESH
BF = jnp.bfloat16
F32 = jnp.float32

OCC, PART, COUP, XM, CM, C2M, T1F, T2F, YM, T1D, T2D, COUNT = 0, 2, 4, 6, 10, 12, 16, 20, 24, 32, 40, 48


def dot(a, b):
    return jnp.dot(a, b, preferred_element_type=F32)


def dot_nt(a, b):
    return lax.dot_general(a, b, (((1,), (1,)), ((), ())), preferred_element_type=F32)


def kernel(
    n, roles,
    three_hbm, coeff_hbm, amps_hbm, occ_hbm, part_hbm, coup_hbm,
    ev_hbm, eo_hbm, nv_hbm, own_hbm,
    out_amp, out_orb,
    b_v, a_v, t_v, x_in, y_out, y_left, y_right, yit_v, s_v, u_v, c_out, c_in, c_own, rm_v, k_v,
    t1_v, t1_f, c2_out, c2_in, t2_v,
    occ_in, part_in, coup_in, w_v,
    ev_ref, eo_ref, nv_ref, occ_ref, part_ref, coup_ref, own_ref,
    load_sem, send_sem, recv_sem,
):
    r = lax.axis_index("role")
    c = lax.axis_index("pairs")
    up, down = lax.rem(r + 1, roles), lax.rem(r + roles - 1, roles)
    naux, npao = b_v.shape[1], b_v.shape[2]
    nv = a_v.shape[2]
    hw = nv // 2
    hr = nv // 2
    pao_scale = 1.0 / math.sqrt(npao)
    aux_scale = 1.0 / math.sqrt(naux)
    virt_scale = 1.0 / math.sqrt(nv)
    y_in = (y_left, y_right)
    near = lax.rem(c, 2)

    def remote(src, dst, base, s_at, r_at, device):
        return pltpu.make_async_remote_copy(
            src_ref=src, dst_ref=dst,
            send_sem=send_sem.at[base + s_at], recv_sem=recv_sem.at[base + r_at],
            device_id=device, device_id_type=MESH,
        )

    def side(d):
        return (r, lax.rem(c + 2 * d - 1 + n, n))

    def level(v):
        return (lax.rem(r + 1 + 2 * v, roles), c)

    def meta(d):
        return (
            remote(occ_hbm, occ_in.at[1 - d], OCC, d, 1 - d, side(d)),
            remote(part_hbm, part_in.at[1 - d], PART, d, 1 - d, side(d)),
            remote(coup_hbm, coup_in.at[1 - d], COUP, d, 1 - d, side(d)),
        )

    def xmsg(d, h):
        cols = pl.ds(h * hw, hw)
        return remote(coeff_hbm.at[r, :, cols], x_in.at[1 - d, :, cols], XM, 2 * d + h, 2 * (1 - d) + h, side(d))

    def ymsg(d, h, k):
        part = pl.ds(k * (naux // 2), naux // 2)
        return remote(
            y_out.at[d, h, part], y_in[h].at[2 * (1 - d), part],
            YM, 4 * d + 2 * h + k, 4 * (1 - d) + 2 * h + k, side(d),
        )

    def cmsg(d):
        return remote(c_out.at[d], c_in.at[1 - d], CM, d, 1 - d, side(d))

    def c2msg(d, h):
        return remote(c2_out.at[d, h], c2_in.at[1 - d, h], C2M, 2 * d + h, 2 * (1 - d) + h, side(d))

    def direct(buf, base, v, h, k):
        part = buf.at[r, h, pl.ds(k * hr, hr)]
        return remote(part, part, base, 4 * v + 2 * h + k, 4 * (1 - v) + 2 * h + k, level(v))

    def forward(buf, base, v, h):
        which = down if v == 0 else up
        part = buf.at[which, h, pl.ds(v * hr, hr)]
        return remote(part, part, base, 2 * v + h, 2 * (1 - v) + h, level(v))

    def spread(buf, base, h):
        for at in range(2):
            for v in range(2):
                direct(buf, base, v, h, v if at == 0 else 1 - v).start()

    def relay(buf, base, again, h):
        for v in range(2):
            direct(buf, base, 1 - v, h, 1 - v).wait_recv()
            forward(buf, again, 1 - v, h).start()

    barrier = pltpu.get_barrier_semaphore()
    for device in (side(0), side(1), level(0), level(1)):
        pl.semaphore_signal(barrier, inc=1, device_id=device, device_id_type=MESH)
    sources = (
        coeff_hbm, three_hbm, amps_hbm, occ_hbm, part_hbm, coup_hbm, ev_hbm, eo_hbm, nv_hbm, own_hbm
    )
    places = (a_v, b_v, t_v, occ_ref, part_ref, coup_ref, ev_ref, eo_ref, nv_ref, own_ref)
    loads = [
        pltpu.make_async_copy(src, dst, load_sem.at[at])
        for at, (src, dst) in enumerate(zip(sources, places))
    ]
    for load in loads[3:] + loads[:3]:
        load.start()
    pl.semaphore_wait(barrier, 4)

    order = (near, 1 - near)
    for d in order:
        meta(d)[0].start()
        xmsg(d, 0).start()
    for d in order:
        for message in meta(d)[1:]:
            message.start()
        xmsg(d, 1).start()

    for load in loads[3:]:
        load.wait()
    second = lax.rem(occ_ref[1, r] - 2 * (c - 1) + 2 * n, 2 * n)
    where_j = jnp.minimum(second // 2, 2)
    i_at = lax.rem(occ_ref[0, r], 2)
    j_at = lax.rem(occ_ref[1, r], 2)
    occ_shift = eo_ref[occ_ref[0, r]] + eo_ref[occ_ref[1, r]]
    count = nv_ref[r]

    def weights(at, parts, coups):
        for q in range(roles):
            total = jnp.float32(0.0)
            for k in range(part_ref.shape[1]):
                total = total + jnp.where(parts(k) == roles * c + q, coups(k), jnp.float32(0.0))
            w_v[at, q] = total

    def overlap(x, at):
        xt = x.T
        for q in range(roles):
            s_v[at, :, q * nv:(q + 1) * nv] = (dot(xt, a_v[q]) * (1.0 / npao)).astype(BF)

    def middle(at, q, amp):
        cols = pl.ds(pl.multiple_of(q * nv, nv), nv)
        u_v[at, :, cols] = (dot(s_v[at, :, cols], amp) * w_v[at, q]).astype(BF)

    def coupled(at):
        return dot_nt(u_v[at], s_v[at])

    def whole(buf, at):
        return jnp.concatenate([buf[at, 0], buf[at, 1]], axis=1)

    rows = lax.broadcasted_iota(jnp.int32, (nv, nv), 0)
    cols = lax.broadcasted_iota(jnp.int32, (nv, nv), 1)
    ev = jnp.broadcast_to(ev_ref[pl.ds(r, 1), :], (nv, nv))
    keep = (rows < count) & (cols < count)
    rm_v[...] = jnp.where(keep, 1.0 / (ev + ev.T - occ_shift + 1.0), 0.0)
    weights(2, lambda k: part_ref[r, k], lambda k: coup_ref[r, k])

    loads[0].wait()
    loads[1].wait()
    own = a_v[r]
    yit_v[...] = (dot(b_v[i_at], own) * pao_scale).astype(BF).T
    loads[2].wait()
    for d in order:
        meta(1 - d)[0].wait_recv()

    far = 1 - near
    half_aux = naux // 2
    near_at = lax.rem(occ_in[near, 1, r], 2)
    far_at = lax.rem(occ_in[far, 1, r], 2)

    def near_half(h):
        x = x_in[near, :, h * hw:(h + 1) * hw]
        for k in range(2):
            part = slice(k * half_aux, (k + 1) * half_aux)
            y_out[near, h, part] = (dot(b_v[near_at, part], x) * pao_scale).astype(BF)
            ymsg(near, h, k).start()

    xmsg(1 - near, 0).wait_recv()
    near_half(0)
    for h in range(2):
        xmsg(1 - far, h).wait_recv()
    y_far = (dot(b_v[far_at], x_in[far]) * pao_scale).astype(BF)
    for h in range(2):
        y_out[far, h] = y_far[:, h * hw:(h + 1) * hw]
    for h in range(2):
        for k in range(2):
            ymsg(far, h, k).start()
    xmsg(1 - near, 1).wait_recv()
    overlap(x_in[near], near)
    for at in (near, far):
        for message in meta(1 - at)[1:]:
            message.wait_recv()
        weights(at, lambda k: part_in[at, r, k], lambda k: coup_in[at, r, k])
        for q in range(roles):
            middle(at, q, t_v[q])
        c_out[at] = coupled(at).astype(BF)
        cmsg(at).start()
        if at is near:
            near_half(1)
            overlap(x_in[far], far)

    yj = (dot(b_v[j_at], own) * pao_scale).astype(BF)
    for h in range(2):
        y_in[h][1] = yj[:, h * hw:(h + 1) * hw]
    overlap(own, 2)
    for q in range(roles):
        middle(2, q, t_v[q])
    c_own[...] = t_v[r].astype(F32) - coupled(2)

    for h in range(2):
        for d in range(2):
            for k in range(2):
                ymsg(d, h, k).wait_recv()
        lanes = slice(h * hw, (h + 1) * hw)
        k1 = dot(yit_v[...], y_in[h][where_j]) * aux_scale
        k_v[:, lanes] = k1
        if h == 0:
            for d in range(2):
                cmsg(d).wait_recv()
            c_own[...] = c_own[...] - c_in[0].astype(F32) - c_in[1].astype(F32)
        fresh = rm_v[:, lanes] * (c_own[:, lanes] - k1)
        t1_v[r, h] = fresh.astype(BF)
        spread(t1_v, T1D, h)
        t1_f[:, lanes] = fresh
    relay(t1_v, T1D, T1F, 0)

    t1 = t1_f[...].astype(BF)
    for at in (near, far, 2):
        middle(at, r, t1)
    half = k_v[...] + dot(k_v[...].astype(BF), t1) * virt_scale
    k2 = half + dot(t1.T, half.astype(BF)) * virt_scale
    k_v[...] = t1_f[...] - k2

    relay(t1_v, T1D, T1F, 1)
    for v in range(2):
        for h in range(2):
            direct(t1_v, T1D, 1 - v, h, v).wait_recv()
    for q in (down, up):
        amp = whole(t1_v, q)
        for at in (near, far, 2):
            middle(at, q, amp)
    for h in range(2):
        for v in range(2):
            forward(t1_v, T1F, v, h).wait_recv()
    across = lax.rem(r + 2, roles)
    amp = whole(t1_v, across)
    for at in (near, far):
        middle(at, across, amp)
        part = coupled(at).astype(BF)
        for h in range(2):
            c2_out[at, h] = part[:, h * hw:(h + 1) * hw]
            c2msg(at, h).start()
    middle(2, across, amp)
    k_v[...] = k_v[...] - coupled(2)

    slots = []
    for s in range(SLOTS):
        pair, found = jnp.int32(0), jnp.int32(0)
        for q in range(roles):
            rank = jnp.int32(0)
            for e in range(q):
                rank = rank + jnp.where(own_ref[e] == own_ref[q], 1, 0)
            hit = jnp.where((own_ref[q] == r) & (rank == s), 1, 0)
            pair = pair + q * hit
            found = found + hit
        slots.append((pair, found.astype(F32)))

    for h in range(2):
        for d in range(2):
            c2msg(d, h).wait_recv()
        lanes = slice(h * hw, (h + 1) * hw)
        total = k_v[:, lanes] - c2_in[0, h].astype(F32) - c2_in[1, h].astype(F32)
        t2_v[r, h] = (rm_v[:, lanes] * total).astype(BF)
        spread(t2_v, T2D, h)
    for h in range(2):
        relay(t2_v, T2D, T2F, h)
    for h in range(2):
        for v in range(2):
            direct(t2_v, T2D, 1 - v, h, v).wait_recv()
    for h in range(2):
        for v in range(2):
            forward(t2_v, T2F, v, h).wait_recv()
    for s, (pair, found) in enumerate(slots):
        amp = whole(t2_v, pair)
        out_amp[s] = (amp.astype(F32) * found).astype(BF)
        orb = a_v[pair]
        out_orb[s] = ((orb.astype(F32) + dot(orb, amp) * virt_scale) * found).astype(BF)

    for d in range(2):
        for message in meta(d):
            message.wait_send()
        cmsg(d).wait_send()
        for h in range(2):
            xmsg(d, h).wait_send()
            c2msg(d, h).wait_send()
            for k in range(2):
                ymsg(d, h, k).wait_send()
            for buf, base, again in ((t1_v, T1D, T1F), (t2_v, T2D, T2F)):
                for k in range(2):
                    direct(buf, base, d, h, k).wait_send()
                forward(buf, again, d, h).wait_send()


def local(three_index, coeff, amps, eps_virt, eps_occ, nvirt, pair_occ, partners, coupling, pair_owner):
    n, roles = lax.axis_size("pairs"), lax.axis_size("role")
    _, naux, npao = three_index.shape
    pairs, _, nv = coeff.shape
    anywhere = pl.BlockSpec(memory_space=pl.ANY)
    vector = pl.BlockSpec(memory_space=pltpu.VMEM)
    hw = nv // 2
    return pl.pallas_call(
        functools.partial(kernel, n, roles),
        out_shape=(
            pltpu.VMEM((SLOTS, nv, nv), BF),
            pltpu.VMEM((SLOTS, npao, nv), BF),
        ),
        in_specs=[anywhere] * 10,
        out_specs=(vector, vector),
        scratch_shapes=[
            pltpu.VMEM(three_index.shape, BF),
            pltpu.VMEM(coeff.shape, BF),
            pltpu.VMEM(amps.shape, BF),
            pltpu.VMEM((2, npao, nv), BF),
            pltpu.VMEM((2, 2, naux, hw), BF),
            pltpu.VMEM((3, naux, hw), BF),
            pltpu.VMEM((3, naux, hw), BF),
            pltpu.VMEM((nv, naux), BF),
            pltpu.VMEM((3, nv, pairs * nv), BF),
            pltpu.VMEM((3, nv, pairs * nv), BF),
            pltpu.VMEM((2, nv, nv), BF),
            pltpu.VMEM((2, nv, nv), BF),
            pltpu.VMEM((nv, nv), F32),
            pltpu.VMEM((nv, nv), F32),
            pltpu.VMEM((nv, nv), F32),
            pltpu.VMEM((pairs, 2, nv, hw), BF),
            pltpu.VMEM((nv, nv), F32),
            pltpu.VMEM((2, 2, nv, hw), BF),
            pltpu.VMEM((2, 2, nv, hw), BF),
            pltpu.VMEM((pairs, 2, nv, hw), BF),
            pltpu.SMEM((2,) + pair_occ.shape[::-1], jnp.int32),
            pltpu.SMEM((2,) + partners.shape, jnp.int32),
            pltpu.SMEM((2,) + coupling.shape, F32),
            pltpu.SMEM((3, pairs), F32),
            pltpu.VMEM(eps_virt.shape, F32),
            pltpu.SMEM(eps_occ.shape, F32),
            pltpu.SMEM(nvirt.shape, jnp.int32),
            pltpu.SMEM(pair_occ.shape[::-1], jnp.int32),
            pltpu.SMEM(partners.shape, jnp.int32),
            pltpu.SMEM(coupling.shape, F32),
            pltpu.SMEM(pair_owner.shape, jnp.int32),
            pltpu.SemaphoreType.DMA((10,)),
            pltpu.SemaphoreType.DMA((COUNT,)),
            pltpu.SemaphoreType.DMA((COUNT,)),
        ],
        compiler_params=pltpu.CompilerParams(
            collective_id=0, has_side_effects=True, vmem_limit_bytes=64 * 1024 * 1024 - 2 * 1024 * 1024
        ),
    )(
        three_index, coeff, amps, pair_occ.T, partners, coupling,
        eps_virt, eps_occ, nvirt, pair_owner,
    )


def solution(mesh):
    in_specs = (
        P("pairs", None, None),
        P("pairs", None, None),
        P("pairs", None, None),
        P("pairs", None),
        P(),
        P("pairs"),
        P("pairs", None),
        P("pairs", None),
        P("pairs", None),
        P("pairs"),
    )
    out_specs = (P(("role", "pairs"), None, None), P(("role", "pairs"), None, None))
    return jax.shard_map(local, mesh=mesh, in_specs=in_specs, out_specs=out_specs, check_vma=False)
```

time: 60.1 us -> 49.5 us (0.82)
  local copies, waits for them, and re-layouts: 10.2 us -> 1.5 us
  Pallas kernels: 48.9 us -> 47.2 us
    unnamed x21 -> x2, local copies, waits for them, and re-layouts: 10.2 us -> 1.5 us
    pallas_call x1, Pallas kernels: 48.9 us -> 47.2 us  [local(): pl.pallas_call(functools.partial(kernel, n, roles), out_shape=(pltpu.VMEM...]
where the time goes in v2:
time: 49.5 us; the launch traced here: 49.4 us
  Pallas kernels  47.2 us (95%)
  local copies, waits for them, and re-layouts  1.5 us (3%)
  between operations  0.64 us (1%)
    pallas_call x1, Pallas kernels, local(): pl.pallas_call(functools.partial(kernel, n, roles), out_shape=(pltpu.VMEM...  47.2 us
    unnamed x2, local copies, waits for them, and re-layouts  1.5 us

profile of v2, /device:TPU:16, one launch (start us, length us, event | category | flops | bytes accessed | tf_op | source)
XLA Modules:
  0.0 49.4 jit_solution(5466605271032287858)
XLA Ops:
  0.6 47.2 %shard_map.113 = (bf16[2,256,256]{2,1,0:T(8,128)(2,1)S(1)}, bf16[2,512,256]{2,1,0:T(8,128)(2,1)S(1)}) custom-call(bf16[2,1024,512]{2,1,0:T(8,128)(2,1)} %three_hbm.1, bf16[4,512,256]{2,1,0:T(8,128)(2,1)} %coeff_hbm.1, bf16[4,256,256]{2,1,0:T(8,128)(2,1)} %amps_hbm.1, s32[2,4]{1,0:T(2,128)} %bitcast.1, s32[4,8]{1,0:T(4,128)} %part_hbm.1, f32[4,8]{1,0:T(4,128)} %coup_hbm.1, ...), custom_call_target="tpu_custom_call" | custom-call | tf_op jit(solution)/shard_map/pallas_call | solution.py:322
  47.9 0.7 %copy.14 = bf16[2,256,256]{2,1,0:T(8,128)(2,1)} copy(bf16[2,256,256]{2,1,0:T(8,128)(2,1)S(1)} %get-tuple-element.2) | data formatting | bytes 524288
  48.6 0.8 %copy.15 = bf16[2,512,256]{2,1,0:T(8,128)(2,1)} copy(bf16[2,512,256]{2,1,0:T(8,128)(2,1)S(1)} %get-tuple-element.3) | data formatting | bytes 1048576

commit v3 on v2

--- a/solution.py
+++ b/solution.py
@@ -13,7 +13,7 @@
 BF = jnp.bfloat16
 F32 = jnp.float32
 
-OCC, PART, COUP, XM, CM, C2M, T1F, T2F, YM, T1D, T2D, COUNT = 0, 2, 4, 6, 10, 12, 16, 20, 24, 32, 40, 48
+OCC, PART, COUP, XM, CM, C2M, YM, T1D, T2D, BM, COUNT = 0, 2, 4, 6, 10, 12, 16, 24, 30, 36, 38
 
 
 def dot(a, b):
@@ -29,7 +29,7 @@
     three_hbm, coeff_hbm, amps_hbm, occ_hbm, part_hbm, coup_hbm,
     ev_hbm, eo_hbm, nv_hbm, own_hbm,
     out_amp, out_orb,
-    b_v, a_v, t_v, x_in, y_out, y_left, y_right, yit_v, s_v, u_v, c_out, c_in, c_own, rm_v, k_v,
+    b_v, a_v, t_v, b_in, x_in, y_out, y_left, y_right, yit_v, s_v, u_v, c_out, c_in, c_own, rm_v, k_v,
     t1_v, t1_f, c2_out, c2_in, t2_v,
     occ_in, part_in, coup_in, w_v,
     ev_ref, eo_ref, nv_ref, occ_ref, part_ref, coup_ref, own_ref,
@@ -37,11 +37,12 @@
 ):
     r = lax.axis_index("role")
     c = lax.axis_index("pairs")
-    up, down = lax.rem(r + 1, roles), lax.rem(r + roles - 1, roles)
+    turn = [lax.rem(r + step, roles) for step in (0, 1, 3, 2)]
     naux, npao = b_v.shape[1], b_v.shape[2]
     nv = a_v.shape[2]
     hw = nv // 2
-    hr = nv // 2
+    raw = naux // 8
+    half_aux = (naux - raw) // 2
     pao_scale = 1.0 / math.sqrt(npao)
     aux_scale = 1.0 / math.sqrt(naux)
     virt_scale = 1.0 / math.sqrt(nv)
@@ -59,21 +60,24 @@
         return (r, lax.rem(c + 2 * d - 1 + n, n))
 
     def level(v):
-        return (lax.rem(r + 1 + 2 * v, roles), c)
+        return (lax.rem(r + 1 + v, roles), c)
 
     def meta(d):
         return (
-            remote(occ_hbm, occ_in.at[1 - d], OCC, d, 1 - d, side(d)),
-            remote(part_hbm, part_in.at[1 - d], PART, d, 1 - d, side(d)),
-            remote(coup_hbm, coup_in.at[1 - d], COUP, d, 1 - d, side(d)),
+            remote(occ_ref, occ_in.at[1 - d], OCC, d, 1 - d, side(d)),
+            remote(part_ref, part_in.at[1 - d], PART, d, 1 - d, side(d)),
+            remote(coup_ref, coup_in.at[1 - d], COUP, d, 1 - d, side(d)),
         )
 
     def xmsg(d, h):
         cols = pl.ds(h * hw, hw)
-        return remote(coeff_hbm.at[r, :, cols], x_in.at[1 - d, :, cols], XM, 2 * d + h, 2 * (1 - d) + h, side(d))
+        return remote(a_v.at[r, :, cols], x_in.at[1 - d, :, cols], XM, 2 * d + h, 2 * (1 - d) + h, side(d))
+
+    def bmsg(d):
+        return remote(b_v.at[:, pl.ds(0, raw)], b_in.at[1 - d], BM, d, 1 - d, side(d))
 
     def ymsg(d, h, k):
-        part = pl.ds(k * (naux // 2), naux // 2)
+        part = pl.ds(raw + k * half_aux, half_aux)
         return remote(
             y_out.at[d, h, part], y_in[h].at[2 * (1 - d), part],
             YM, 4 * d + 2 * h + k, 4 * (1 - d) + 2 * h + k, side(d),
@@ -85,27 +89,15 @@
     def c2msg(d, h):
         return remote(c2_out.at[d, h], c2_in.at[1 - d, h], C2M, 2 * d + h, 2 * (1 - d) + h, side(d))
 
-    def direct(buf, base, v, h, k):
-        part = buf.at[r, h, pl.ds(k * hr, hr)]
-        return remote(part, part, base, 4 * v + 2 * h + k, 4 * (1 - v) + 2 * h + k, level(v))
-
-    def forward(buf, base, v, h):
-        which = down if v == 0 else up
-        part = buf.at[which, h, pl.ds(v * hr, hr)]
-        return remote(part, part, base, 2 * v + h, 2 * (1 - v) + h, level(v))
+    def direct(buf, base, v, h):
+        return remote(buf.at[r, h], buf.at[r, h], base, 2 * v + h, 2 * (2 - v) + h, level(v))
 
     def spread(buf, base, h):
-        for at in range(2):
-            for v in range(2):
-                direct(buf, base, v, h, v if at == 0 else 1 - v).start()
-
-    def relay(buf, base, again, h):
-        for v in range(2):
-            direct(buf, base, 1 - v, h, 1 - v).wait_recv()
-            forward(buf, again, 1 - v, h).start()
+        for v in (1, 0, 2):
+            direct(buf, base, v, h).start()
 
     barrier = pltpu.get_barrier_semaphore()
-    for device in (side(0), side(1), level(0), level(1)):
+    for device in (side(near), side(1 - near), level(0), level(1), level(2)):
         pl.semaphore_signal(barrier, inc=1, device_id=device, device_id_type=MESH)
     sources = (
         coeff_hbm, three_hbm, amps_hbm, occ_hbm, part_hbm, coup_hbm, ev_hbm, eo_hbm, nv_hbm, own_hbm
@@ -117,9 +109,11 @@
     ]
     for load in loads[3:] + loads[:3]:
         load.start()
-    pl.semaphore_wait(barrier, 4)
+    pl.semaphore_wait(barrier, 5)
 
     order = (near, 1 - near)
+    for load in loads[3:] + loads[:1]:
+        load.wait()
     for d in order:
         meta(d)[0].start()
         xmsg(d, 0).start()
@@ -127,9 +121,10 @@
         for message in meta(d)[1:]:
             message.start()
         xmsg(d, 1).start()
-
-    for load in loads[3:]:
-        load.wait()
+    loads[1].wait()
+    for d in order:
+        bmsg(d).start()
+
     second = lax.rem(occ_ref[1, r] - 2 * (c - 1) + 2 * n, 2 * n)
     where_j = jnp.minimum(second // 2, 2)
     i_at = lax.rem(occ_ref[0, r], 2)
@@ -146,15 +141,16 @@
 
     def overlap(x, at):
         xt = x.T
-        for q in range(roles):
-            s_v[at, :, q * nv:(q + 1) * nv] = (dot(xt, a_v[q]) * (1.0 / npao)).astype(BF)
-
-    def middle(at, q, amp):
-        cols = pl.ds(pl.multiple_of(q * nv, nv), nv)
-        u_v[at, :, cols] = (dot(s_v[at, :, cols], amp) * w_v[at, q]).astype(BF)
-
-    def coupled(at):
-        return dot_nt(u_v[at], s_v[at])
+        for k, q in enumerate(turn):
+            s_v[at, :, k * nv:(k + 1) * nv] = (dot(xt, a_v[q]) * (1.0 / npao)).astype(BF)
+
+    def middle(at, k, amp):
+        lanes = slice(k * nv, (k + 1) * nv)
+        u_v[at, :, lanes] = (dot(s_v[at, :, lanes], amp) * w_v[at, turn[k]]).astype(BF)
+
+    def coupled(at, first=0, last=roles):
+        lanes = slice(first * nv, last * nv)
+        return dot_nt(u_v[at, :, lanes], s_v[at, :, lanes])
 
     def whole(buf, at):
         return jnp.concatenate([buf[at, 0], buf[at, 1]], axis=1)
@@ -166,8 +162,6 @@
     rm_v[...] = jnp.where(keep, 1.0 / (ev + ev.T - occ_shift + 1.0), 0.0)
     weights(2, lambda k: part_ref[r, k], lambda k: coup_ref[r, k])
 
-    loads[0].wait()
-    loads[1].wait()
     own = a_v[r]
     yit_v[...] = (dot(b_v[i_at], own) * pao_scale).astype(BF).T
     loads[2].wait()
@@ -175,14 +169,13 @@
         meta(1 - d)[0].wait_recv()
 
     far = 1 - near
-    half_aux = naux // 2
     near_at = lax.rem(occ_in[near, 1, r], 2)
     far_at = lax.rem(occ_in[far, 1, r], 2)
 
     def near_half(h):
         x = x_in[near, :, h * hw:(h + 1) * hw]
         for k in range(2):
-            part = slice(k * half_aux, (k + 1) * half_aux)
+            part = slice(raw + k * half_aux, raw + (k + 1) * half_aux)
             y_out[near, h, part] = (dot(b_v[near_at, part], x) * pao_scale).astype(BF)
             ymsg(near, h, k).start()
 
@@ -190,9 +183,9 @@
     near_half(0)
     for h in range(2):
         xmsg(1 - far, h).wait_recv()
-    y_far = (dot(b_v[far_at], x_in[far]) * pao_scale).astype(BF)
-    for h in range(2):
-        y_out[far, h] = y_far[:, h * hw:(h + 1) * hw]
+    y_far = (dot(b_v[far_at, raw:], x_in[far]) * pao_scale).astype(BF)
+    for h in range(2):
+        y_out[far, h, raw:] = y_far[:, h * hw:(h + 1) * hw]
     for h in range(2):
         for k in range(2):
             ymsg(far, h, k).start()
@@ -202,8 +195,8 @@
         for message in meta(1 - at)[1:]:
             message.wait_recv()
         weights(at, lambda k: part_in[at, r, k], lambda k: coup_in[at, r, k])
-        for q in range(roles):
-            middle(at, q, t_v[q])
+        for k, q in enumerate(turn):
+            middle(at, k, t_v[q])
         c_out[at] = coupled(at).astype(BF)
         cmsg(at).start()
         if at is near:
@@ -213,9 +206,15 @@
     yj = (dot(b_v[j_at], own) * pao_scale).astype(BF)
     for h in range(2):
         y_in[h][1] = yj[:, h * hw:(h + 1) * hw]
+    for d in range(2):
+        bmsg(d).wait_recv()
+    for d in range(2):
+        yb = (dot(b_in[d, j_at], own) * pao_scale).astype(BF)
+        for h in range(2):
+            y_in[h][2 * d, :raw] = yb[:, h * hw:(h + 1) * hw]
     overlap(own, 2)
-    for q in range(roles):
-        middle(2, q, t_v[q])
+    for k, q in enumerate(turn):
+        middle(2, k, t_v[q])
     c_own[...] = t_v[r].astype(F32) - coupled(2)
 
     for h in range(2):
@@ -233,36 +232,49 @@
         t1_v[r, h] = fresh.astype(BF)
         spread(t1_v, T1D, h)
         t1_f[:, lanes] = fresh
-    relay(t1_v, T1D, T1F, 0)
 
     t1 = t1_f[...].astype(BF)
     for at in (near, far, 2):
-        middle(at, r, t1)
+        middle(at, 0, t1)
     half = k_v[...] + dot(k_v[...].astype(BF), t1) * virt_scale
     k2 = half + dot(t1.T, half.astype(BF)) * virt_scale
     k_v[...] = t1_f[...] - k2
 
-    relay(t1_v, T1D, T1F, 1)
-    for v in range(2):
-        for h in range(2):
-            direct(t1_v, T1D, 1 - v, h, v).wait_recv()
-    for q in (down, up):
-        amp = whole(t1_v, q)
-        for at in (near, far, 2):
-            middle(at, q, amp)
-    for h in range(2):
-        for v in range(2):
-            forward(t1_v, T1F, v, h).wait_recv()
-    across = lax.rem(r + 2, roles)
-    amp = whole(t1_v, across)
-    for at in (near, far):
-        middle(at, across, amp)
-        part = coupled(at).astype(BF)
-        for h in range(2):
-            c2_out[at, h] = part[:, h * hw:(h + 1) * hw]
+    def arrived(buf, base, k):
+        for h in range(2):
+            direct(buf, base, (None, 2, 0, 1)[k], h).wait_recv()
+
+    def send_c2(at, part):
+        for h in range(2):
+            c2_out[at, h] = part[:, h * hw:(h + 1) * hw].astype(BF)
             c2msg(at, h).start()
-    middle(2, across, amp)
+
+    for k in (1, 2):
+        arrived(t1_v, T1D, k)
+        middle(near, k, whole(t1_v, turn[k]))
+    t1_f[...] = coupled(near, 0, 3)
+    arrived(t1_v, T1D, 3)
+    middle(near, 3, whole(t1_v, turn[3]))
+    send_c2(near, t1_f[...] + coupled(near, 3, 4))
+    for k in (1, 2, 3):
+        middle(far, k, whole(t1_v, turn[k]))
+    send_c2(far, coupled(far))
+    for k in (1, 2, 3):
+        middle(2, k, whole(t1_v, turn[k]))
     k_v[...] = k_v[...] - coupled(2)
+
+    for d in range(2):
+        for message in meta(d):
+            message.wait_send()
+        cmsg(d).wait_send()
+        bmsg(d).wait_send()
+        for h in range(2):
+            xmsg(d, h).wait_send()
+            for k in range(2):
+                ymsg(d, h, k).wait_send()
+    for v in range(3):
+        for h in range(2):
+            direct(t1_v, T1D, v, h).wait_send()
 
     slots = []
     for s in range(SLOTS):
@@ -283,33 +295,19 @@
         total = k_v[:, lanes] - c2_in[0, h].astype(F32) - c2_in[1, h].astype(F32)
         t2_v[r, h] = (rm_v[:, lanes] * total).astype(BF)
         spread(t2_v, T2D, h)
-    for h in range(2):
-        relay(t2_v, T2D, T2F, h)
-    for h in range(2):
-        for v in range(2):
-            direct(t2_v, T2D, 1 - v, h, v).wait_recv()
-    for h in range(2):
-        for v in range(2):
-            forward(t2_v, T2F, v, h).wait_recv()
+    for k in (1, 2, 3):
+        arrived(t2_v, T2D, k)
     for s, (pair, found) in enumerate(slots):
         amp = whole(t2_v, pair)
         out_amp[s] = (amp.astype(F32) * found).astype(BF)
         orb = a_v[pair]
         out_orb[s] = ((orb.astype(F32) + dot(orb, amp) * virt_scale) * found).astype(BF)
 
-    for d in range(2):
-        for message in meta(d):
-            message.wait_send()
-        cmsg(d).wait_send()
-        for h in range(2):
-            xmsg(d, h).wait_send()
+    for h in range(2):
+        for d in range(2):
             c2msg(d, h).wait_send()
-            for k in range(2):
-                ymsg(d, h, k).wait_send()
-            for buf, base, again in ((t1_v, T1D, T1F), (t2_v, T2D, T2F)):
-                for k in range(2):
-                    direct(buf, base, d, h, k).wait_send()
-                forward(buf, again, d, h).wait_send()
+        for v in range(3):
+            direct(t2_v, T2D, v, h).wait_send()
 
 
 def local(three_index, coeff, amps, eps_virt, eps_occ, nvirt, pair_occ, partners, coupling, pair_owner):
@@ -331,6 +329,7 @@
             pltpu.VMEM(three_index.shape, BF),
             pltpu.VMEM(coeff.shape, BF),
             pltpu.VMEM(amps.shape, BF),
+            pltpu.VMEM((2, 2, naux // 8, npao), BF),
             pltpu.VMEM((2, npao, nv), BF),
             pltpu.VMEM((2, 2, naux, hw), BF),
             pltpu.VMEM((3, naux, hw), BF),

time: 49.5 us -> 46.6 us (0.941)
  the two profiles are of different devices: /device:TPU:16 before, /device:TPU:8 now
where the time goes in v3:
time: 46.6 us; the launch traced here: 46.5 us
  Pallas kernels  44.3 us (95%)
  local copies, waits for them, and re-layouts  1.5 us (3%)
  between operations  0.64 us (1%)
    pallas_call x1, Pallas kernels, local(): pl.pallas_call(functools.partial(kernel, n, roles), out_shape=(pltpu.VMEM...  44.3 us
    unnamed x2, local copies, waits for them, and re-layouts  1.5 us

profile of v3, /device:TPU:8, one launch (start us, length us, event | category | flops | bytes accessed | tf_op | source)
XLA Modules:
  0.0 46.5 jit_solution(4692106200147982424)
XLA Ops:
  0.6 44.3 %shard_map.113 = (bf16[2,256,256]{2,1,0:T(8,128)(2,1)S(1)}, bf16[2,512,256]{2,1,0:T(8,128)(2,1)S(1)}) custom-call(bf16[2,1024,512]{2,1,0:T(8,128)(2,1)} %three_hbm.1, bf16[4,512,256]{2,1,0:T(8,128)(2,1)} %coeff_hbm.1, bf16[4,256,256]{2,1,0:T(8,128)(2,1)} %amps_hbm.1, s32[2,4]{1,0:T(2,128)} %bitcast.1, s32[4,8]{1,0:T(4,128)} %part_hbm.1, f32[4,8]{1,0:T(4,128)} %coup_hbm.1, ...), custom_call_target="tpu_custom_call" | custom-call | tf_op jit(solution)/shard_map/pallas_call | solution.py:320
  45.0 0.7 %copy.14 = bf16[2,256,256]{2,1,0:T(8,128)(2,1)} copy(bf16[2,256,256]{2,1,0:T(8,128)(2,1)S(1)} %get-tuple-element.2) | data formatting | bytes 524288
  45.7 0.8 %copy.15 = bf16[2,512,256]{2,1,0:T(8,128)(2,1)} copy(bf16[2,512,256]{2,1,0:T(8,128)(2,1)S(1)} %get-tuple-element.3) | data formatting | bytes 1048576

commit v4 on v3

--- a/solution.py
+++ b/solution.py
@@ -13,7 +13,7 @@
 BF = jnp.bfloat16
 F32 = jnp.float32
 
-OCC, PART, COUP, XM, CM, C2M, YM, T1D, T2D, BM, COUNT = 0, 2, 4, 6, 10, 12, 16, 24, 30, 36, 38
+OCC, PART, COUP, XM, CM, C2M, YM, T1D, T2D, BM, OWN, COUNT = 0, 2, 4, 6, 10, 12, 16, 24, 30, 36, 38, 40
 
 
 def dot(a, b):
@@ -30,8 +30,8 @@
     ev_hbm, eo_hbm, nv_hbm, own_hbm,
     out_amp, out_orb,
     b_v, a_v, t_v, b_in, x_in, y_out, y_left, y_right, yit_v, s_v, u_v, c_out, c_in, c_own, rm_v, k_v,
-    t1_v, t1_f, c2_out, c2_in, t2_v,
-    occ_in, part_in, coup_in, w_v,
+    t1_v, t1_f, c2_out, c2_in, t2_out, t2_in, x_out,
+    occ_in, part_in, coup_in, own_in, w_v,
     ev_ref, eo_ref, nv_ref, occ_ref, part_ref, coup_ref, own_ref,
     load_sem, send_sem, recv_sem,
 ):
@@ -67,11 +67,12 @@
             remote(occ_ref, occ_in.at[1 - d], OCC, d, 1 - d, side(d)),
             remote(part_ref, part_in.at[1 - d], PART, d, 1 - d, side(d)),
             remote(coup_ref, coup_in.at[1 - d], COUP, d, 1 - d, side(d)),
+            remote(own_ref, own_in.at[1 - d], OWN, d, 1 - d, side(d)),
         )
 
     def xmsg(d, h):
         cols = pl.ds(h * hw, hw)
-        return remote(a_v.at[r, :, cols], x_in.at[1 - d, :, cols], XM, 2 * d + h, 2 * (1 - d) + h, side(d))
+        return remote(x_out.at[:, cols], x_in.at[1 - d, :, cols], XM, 2 * d + h, 2 * (1 - d) + h, side(d))
 
     def bmsg(d):
         return remote(b_v.at[:, pl.ds(0, raw)], b_in.at[1 - d], BM, d, 1 - d, side(d))
@@ -95,6 +96,19 @@
     def spread(buf, base, h):
         for v in (1, 0, 2):
             direct(buf, base, v, h).start()
+
+    def last(v, h):
+        return remote(t2_out.at[h], t2_in.at[h], T2D, 2 * v + h, h, level(v))
+
+    def pair_of(owner, role):
+        found = jnp.int32(0)
+        for q in range(roles):
+            rank = jnp.int32(0)
+            for e in range(q):
+                rank = rank + jnp.where(owner(e) == owner(q), 1, 0)
+            first = (owner(q) == role) & (rank == 0) & (role > 0)
+            found = found + jnp.where(first | ((role == 0) & (rank == 1)), q, 0)
+        return found
 
     barrier = pltpu.get_barrier_semaphore()
     for device in (side(near), side(1 - near), level(0), level(1), level(2)):
@@ -109,28 +123,32 @@
     ]
     for load in loads[3:] + loads[:3]:
         load.start()
-    pl.semaphore_wait(barrier, 5)
-
-    order = (near, 1 - near)
     for load in loads[3:] + loads[:1]:
         load.wait()
+    pairs = [pair_of(lambda e: own_ref[e], role) for role in turn]
+    mine = pairs[0]
+    x_out[...] = a_v[mine]
+    pl.semaphore_wait(barrier, 5)
+
+    order = (near, 1 - near)
     for d in order:
         meta(d)[0].start()
+        meta(d)[3].start()
         xmsg(d, 0).start()
     for d in order:
-        for message in meta(d)[1:]:
+        for message in meta(d)[1:3]:
             message.start()
         xmsg(d, 1).start()
     loads[1].wait()
     for d in order:
         bmsg(d).start()
 
-    second = lax.rem(occ_ref[1, r] - 2 * (c - 1) + 2 * n, 2 * n)
+    second = lax.rem(occ_ref[1, mine] - 2 * (c - 1) + 2 * n, 2 * n)
     where_j = jnp.minimum(second // 2, 2)
-    i_at = lax.rem(occ_ref[0, r], 2)
-    j_at = lax.rem(occ_ref[1, r], 2)
-    occ_shift = eo_ref[occ_ref[0, r]] + eo_ref[occ_ref[1, r]]
-    count = nv_ref[r]
+    i_at = lax.rem(occ_ref[0, mine], 2)
+    j_at = lax.rem(occ_ref[1, mine], 2)
+    occ_shift = eo_ref[occ_ref[0, mine]] + eo_ref[occ_ref[1, mine]]
+    count = nv_ref[mine]
 
     def weights(at, parts, coups):
         for q in range(roles):
@@ -141,12 +159,12 @@
 
     def overlap(x, at):
         xt = x.T
-        for k, q in enumerate(turn):
+        for k, q in enumerate(pairs):
             s_v[at, :, k * nv:(k + 1) * nv] = (dot(xt, a_v[q]) * (1.0 / npao)).astype(BF)
 
     def middle(at, k, amp):
         lanes = slice(k * nv, (k + 1) * nv)
-        u_v[at, :, lanes] = (dot(s_v[at, :, lanes], amp) * w_v[at, turn[k]]).astype(BF)
+        u_v[at, :, lanes] = (dot(s_v[at, :, lanes], amp) * w_v[at, pairs[k]]).astype(BF)
 
     def coupled(at, first=0, last=roles):
         lanes = slice(first * nv, last * nv)
@@ -157,20 +175,23 @@
 
     rows = lax.broadcasted_iota(jnp.int32, (nv, nv), 0)
     cols = lax.broadcasted_iota(jnp.int32, (nv, nv), 1)
-    ev = jnp.broadcast_to(ev_ref[pl.ds(r, 1), :], (nv, nv))
+    ev = jnp.broadcast_to(ev_ref[pl.ds(mine, 1), :], (nv, nv))
     keep = (rows < count) & (cols < count)
     rm_v[...] = jnp.where(keep, 1.0 / (ev + ev.T - occ_shift + 1.0), 0.0)
-    weights(2, lambda k: part_ref[r, k], lambda k: coup_ref[r, k])
-
-    own = a_v[r]
+    weights(2, lambda k: part_ref[mine, k], lambda k: coup_ref[mine, k])
+
+    own = a_v[mine]
     yit_v[...] = (dot(b_v[i_at], own) * pao_scale).astype(BF).T
     loads[2].wait()
     for d in order:
         meta(1 - d)[0].wait_recv()
+        meta(1 - d)[3].wait_recv()
 
     far = 1 - near
-    near_at = lax.rem(occ_in[near, 1, r], 2)
-    far_at = lax.rem(occ_in[far, 1, r], 2)
+    near_pair = pair_of(lambda e: own_in[near, e], r)
+    far_pair = pair_of(lambda e: own_in[far, e], r)
+    near_at = lax.rem(occ_in[near, 1, near_pair], 2)
+    far_at = lax.rem(occ_in[far, 1, far_pair], 2)
 
     def near_half(h):
         x = x_in[near, :, h * hw:(h + 1) * hw]
@@ -191,11 +212,12 @@
             ymsg(far, h, k).start()
     xmsg(1 - near, 1).wait_recv()
     overlap(x_in[near], near)
-    for at in (near, far):
-        for message in meta(1 - at)[1:]:
+    for d in order:
+        for message in meta(1 - d)[1:3]:
             message.wait_recv()
-        weights(at, lambda k: part_in[at, r, k], lambda k: coup_in[at, r, k])
-        for k, q in enumerate(turn):
+    for at, pair in ((near, near_pair), (far, far_pair)):
+        weights(at, lambda k: part_in[at, pair, k], lambda k: coup_in[at, pair, k])
+        for k, q in enumerate(pairs):
             middle(at, k, t_v[q])
         c_out[at] = coupled(at).astype(BF)
         cmsg(at).start()
@@ -213,9 +235,9 @@
         for h in range(2):
             y_in[h][2 * d, :raw] = yb[:, h * hw:(h + 1) * hw]
     overlap(own, 2)
-    for k, q in enumerate(turn):
+    for k, q in enumerate(pairs):
         middle(2, k, t_v[q])
-    c_own[...] = t_v[r].astype(F32) - coupled(2)
+    c_own[...] = t_v[mine].astype(F32) - coupled(2)
 
     for h in range(2):
         for d in range(2):
@@ -276,38 +298,45 @@
         for h in range(2):
             direct(t1_v, T1D, v, h).wait_send()
 
-    slots = []
-    for s in range(SLOTS):
-        pair, found = jnp.int32(0), jnp.int32(0)
-        for q in range(roles):
-            rank = jnp.int32(0)
-            for e in range(q):
-                rank = rank + jnp.where(own_ref[e] == own_ref[q], 1, 0)
-            hit = jnp.where((own_ref[q] == r) & (rank == s), 1, 0)
-            pair = pair + q * hit
-            found = found + hit
-        slots.append((pair, found.astype(F32)))
-
     for h in range(2):
         for d in range(2):
             c2msg(d, h).wait_recv()
         lanes = slice(h * hw, (h + 1) * hw)
         total = k_v[:, lanes] - c2_in[0, h].astype(F32) - c2_in[1, h].astype(F32)
-        t2_v[r, h] = (rm_v[:, lanes] * total).astype(BF)
-        spread(t2_v, T2D, h)
-    for k in (1, 2, 3):
-        arrived(t2_v, T2D, k)
-    for s, (pair, found) in enumerate(slots):
-        amp = whole(t2_v, pair)
-        out_amp[s] = (amp.astype(F32) * found).astype(BF)
+        t2_out[h] = (rm_v[:, lanes] * total).astype(BF)
+
+        @pl.when(r == 0)
+        def _():
+            for v in (1, 0, 2):
+                last(v, h).start()
+
+    def emit(slot, buf, pair, found):
+        amp = jnp.concatenate([buf[0], buf[1]], axis=1)
+        out_amp[slot] = (amp.astype(F32) * found).astype(BF)
         orb = a_v[pair]
-        out_orb[s] = ((orb.astype(F32) + dot(orb, amp) * virt_scale) * found).astype(BF)
+        out_orb[slot] = ((orb.astype(F32) + dot(orb, amp) * virt_scale) * found).astype(BF)
+
+    emit(0, t2_out, mine, jnp.where(r > 0, jnp.float32(1.0), jnp.float32(0.0)))
+    second_pair = pair_of(lambda e: own_ref[e], jnp.int32(0))
+    held = jnp.where(own_ref[second_pair] == r, jnp.float32(1.0), jnp.float32(0.0))
+
+    @pl.when(r > 0)
+    def _():
+        for h in range(2):
+            last(0, h).wait_recv()
+        emit(1, t2_in, second_pair, held)
+
+    @pl.when(r == 0)
+    def _():
+        out_amp[1] = jnp.zeros_like(out_amp[1])
+        out_orb[1] = jnp.zeros_like(out_orb[1])
+        for h in range(2):
+            for v in range(3):
+                last(v, h).wait_send()
 
     for h in range(2):
         for d in range(2):
             c2msg(d, h).wait_send()
-        for v in range(3):
-            direct(t2_v, T2D, v, h).wait_send()
 
 
 def local(three_index, coeff, amps, eps_virt, eps_occ, nvirt, pair_occ, partners, coupling, pair_owner):
@@ -346,10 +375,13 @@
             pltpu.VMEM((nv, nv), F32),
             pltpu.VMEM((2, 2, nv, hw), BF),
             pltpu.VMEM((2, 2, nv, hw), BF),
-            pltpu.VMEM((pairs, 2, nv, hw), BF),
+            pltpu.VMEM((2, nv, hw), BF),
+            pltpu.VMEM((2, nv, hw), BF),
+            pltpu.VMEM((npao, nv), BF),
             pltpu.SMEM((2,) + pair_occ.shape[::-1], jnp.int32),
             pltpu.SMEM((2,) + partners.shape, jnp.int32),
             pltpu.SMEM((2,) + coupling.shape, F32),
+            pltpu.SMEM((2,) + pair_owner.shape, jnp.int32),
             pltpu.SMEM((3, pairs), F32),
             pltpu.VMEM(eps_virt.shape, F32),
             pltpu.SMEM(eps_occ.shape, F32),

time: 46.6 us -> 46.3 us (level)
  no operation moved by 1% of the time
where the time goes in v4:
time: 46.3 us; the launch traced here: 46.2 us
  Pallas kernels  44.1 us (95%)
  local copies, waits for them, and re-layouts  1.5 us (3%)
  between operations  0.64 us (1%)
    pallas_call x1, Pallas kernels, local(): pl.pallas_call(functools.partial(kernel, n, roles), out_shape=(pltpu.VMEM...  44.1 us
    unnamed x2, local copies, waits for them, and re-layouts  1.5 us

profile of v4, /device:TPU:8, one launch (start us, length us, event | category | flops | bytes accessed | tf_op | source)
XLA Modules:
  0.0 46.2 jit_solution(6069351974463553049)
XLA Ops:
  0.6 44.1 %shard_map.113 = (bf16[2,256,256]{2,1,0:T(8,128)(2,1)S(1)}, bf16[2,512,256]{2,1,0:T(8,128)(2,1)S(1)}) custom-call(bf16[2,1024,512]{2,1,0:T(8,128)(2,1)} %three_hbm.1, bf16[4,512,256]{2,1,0:T(8,128)(2,1)} %coeff_hbm.1, bf16[4,256,256]{2,1,0:T(8,128)(2,1)} %amps_hbm.1, s32[2,4]{1,0:T(2,128)} %bitcast.1, s32[4,8]{1,0:T(4,128)} %part_hbm.1, f32[4,8]{1,0:T(4,128)} %coup_hbm.1, ...), custom_call_target="tpu_custom_call" | custom-call | tf_op jit(solution)/shard_map/pallas_call | solution.py:349
  44.7 0.7 %copy.14 = bf16[2,256,256]{2,1,0:T(8,128)(2,1)} copy(bf16[2,256,256]{2,1,0:T(8,128)(2,1)S(1)} %get-tuple-element.2) | data formatting | bytes 524288
  45.4 0.8 %copy.15 = bf16[2,512,256]{2,1,0:T(8,128)(2,1)} copy(bf16[2,512,256]{2,1,0:T(8,128)(2,1)S(1)} %get-tuple-element.3) | data formatting | bytes 1048576

commit v5 on v4

--- a/solution.py
+++ b/solution.py
@@ -41,7 +41,7 @@
     naux, npao = b_v.shape[1], b_v.shape[2]
     nv = a_v.shape[2]
     hw = nv // 2
-    raw = naux // 8
+    raw = naux // 16
     half_aux = (naux - raw) // 2
     pao_scale = 1.0 / math.sqrt(npao)
     aux_scale = 1.0 / math.sqrt(naux)
@@ -358,7 +358,7 @@
             pltpu.VMEM(three_index.shape, BF),
             pltpu.VMEM(coeff.shape, BF),
             pltpu.VMEM(amps.shape, BF),
-            pltpu.VMEM((2, 2, naux // 8, npao), BF),
+            pltpu.VMEM((2, 2, naux // 16, npao), BF),
             pltpu.VMEM((2, npao, nv), BF),
             pltpu.VMEM((2, 2, naux, hw), BF),
             pltpu.VMEM((3, naux, hw), BF),

time: 46.3 us -> 46.7 us (level)
  no operation moved by 1% of the time
where the time goes in v5:
time: 46.7 us; the launch traced here: 46.6 us
  Pallas kernels  44.5 us (95%)
  local copies, waits for them, and re-layouts  1.5 us (3%)
  between operations  0.64 us (1%)
    pallas_call x1, Pallas kernels, local(): pl.pallas_call(functools.partial(kernel, n, roles), out_shape=(pltpu.VMEM...  44.5 us
    unnamed x2, local copies, waits for them, and re-layouts  1.5 us

profile of v5, /device:TPU:8, one launch (start us, length us, event | category | flops | bytes accessed | tf_op | source)
XLA Modules:
  0.0 46.6 jit_solution(12574165841266558760)
XLA Ops:
  0.6 44.5 %shard_map.113 = (bf16[2,256,256]{2,1,0:T(8,128)(2,1)S(1)}, bf16[2,512,256]{2,1,0:T(8,128)(2,1)S(1)}) custom-call(bf16[2,1024,512]{2,1,0:T(8,128)(2,1)} %three_hbm.1, bf16[4,512,256]{2,1,0:T(8,128)(2,1)} %coeff_hbm.1, bf16[4,256,256]{2,1,0:T(8,128)(2,1)} %amps_hbm.1, s32[2,4]{1,0:T(2,128)} %bitcast.1, s32[4,8]{1,0:T(4,128)} %part_hbm.1, f32[4,8]{1,0:T(4,128)} %coup_hbm.1, ...), custom_call_target="tpu_custom_call" | custom-call | tf_op jit(solution)/shard_map/pallas_call | solution.py:349
  45.1 0.7 %copy.14 = bf16[2,256,256]{2,1,0:T(8,128)(2,1)} copy(bf16[2,256,256]{2,1,0:T(8,128)(2,1)S(1)} %get-tuple-element.2) | data formatting | bytes 524288
  45.8 0.8 %copy.15 = bf16[2,512,256]{2,1,0:T(8,128)(2,1)} copy(bf16[2,512,256]{2,1,0:T(8,128)(2,1)S(1)} %get-tuple-element.3) | data formatting | bytes 1048576
